TPU v7x, 128 devices: a whole 4x4x4 slice. The times are simulated.
128 devices in a mesh: patch: 8 (over z, core), mode: 16 (over x, y).
Axes of the slice: x: 4, y: 4, z: 4, core: 2. Of those that a mesh axis runs over, the one named last changes fastest.
Arguments:
- sky_map: bfloat16 [64, 8192, 64], P('patch', 'mode'), may hold values from -6 to 6
- pixel_mask: int32 [64, 8192], P('patch', 'mode'), may hold values 0 or 1
- noise_factor: float32 [64, 16, 64, 64], P('patch', 'mode'), as said below
- cycle_legendre: float32 [64, 6144, 8], P('patch', 'mode'), may hold values from -6 to 6
- band_power: float32 [6144, 8], P('mode', 'patch'), may hold values from 0.1 to 10
- channel_cov: float32 [64, 64], replicated
- test_matrix: bfloat16 [8, 6144, 2, 512], P('patch', 'mode'), may hold values from -6 to 6
Outputs:
- sketch: float32 [64, 512], P(None, ('patch', 'mode'))
Inputs may be any that keep to these rules, and one draw needn't show every extreme that they name: `noise_factor`: each noise factor is lower triangular with a positive diagonal.
All inputs are finite; a program needn't handle non-finite values. No bound on the sum of `pixel_mask` on one device may be relied on, other than what follows from the above.
Results may differ from a plain program's by a relative error of at most 0.017.
Values may be sent and summed in bfloat16 or wider, within the bound.
A program may use at most 64 MiB of HBM per device.

v0:
```python
import math

import jax
import jax.numpy as jnp
from jax import lax
from jax.sharding import PartitionSpec as P


def tables(mode_start, mode_rows, pixel_rows, cycle_pixels):
    modes = mode_start + lax.iota(jnp.int32, mode_rows)
    pixels = lax.iota(jnp.int32, pixel_rows)
    phase = modes[:, None] * pixels[None, :] % cycle_pixels
    angle = phase.astype(jnp.float32) * (2.0 * math.pi / cycle_pixels)
    return (jnp.cos(angle).astype(jnp.bfloat16), jnp.sin(angle).astype(jnp.bfloat16))


def fourier(mode_start, mode_rows, values, cycle_pixels):
    cosine, sine = tables(mode_start, mode_rows, values.shape[0], cycle_pixels)
    real_part = jnp.dot(cosine, values, preferred_element_type=jnp.float32)
    imag_part = -jnp.dot(sine, values, preferred_element_type=jnp.float32)
    return jnp.concatenate([real_part, imag_part], axis=1)


def local(sky_map, pixel_mask, noise_factor, cycle_legendre, band_power, channel_cov, test_matrix):
    cycle_count, pixel_count, chans = sky_map.shape
    mode_count, offset_count = band_power.shape
    mode_devices = lax.axis_size("mode")
    cycle_pixels = pixel_count * mode_devices
    white = jnp.einsum(
        "rdc,rjc->rjd",
        noise_factor[:, 0],
        sky_map.astype(jnp.float32),
        precision=lax.Precision.HIGHEST,
    )
    whitened = (white * pixel_mask.astype(jnp.float32)[:, :, None]).astype(jnp.bfloat16)
    by_pixel = jnp.transpose(whitened, (1, 0, 2))
    flat_pixels = by_pixel.reshape(pixel_count, cycle_count * chans)
    mode_start = lax.axis_index("mode") * mode_count
    four = fourier(
        mode_start,
        mode_count,
        lax.all_gather(flat_pixels, "mode", axis=0, tiled=True),
        cycle_pixels,
    )
    four = four.reshape(mode_count, 2, cycle_count, chans)
    alm = lax.psum_scatter(
        jnp.einsum("rmk,mtrc->kmtc", cycle_legendre, four, precision=lax.Precision.HIGHEST).astype(
            jnp.bfloat16
        ),
        "patch",
        scatter_dimension=0,
        tiled=True,
    ).astype(jnp.float32)
    mixed = jnp.einsum("dc,kmtc->kmtd", channel_cov, alm, precision=lax.Precision.HIGHEST)
    scaled = (mixed * jnp.transpose(band_power)[:, :, None, None]).astype(jnp.bfloat16)
    left = scaled.reshape(-1, chans)
    right = test_matrix.reshape(-1, test_matrix.shape[3])
    partial_sketch = jnp.einsum("pc,ps->cs", left, right, preferred_element_type=jnp.float32)
    return lax.psum_scatter(partial_sketch, ("patch", "mode"), scatter_dimension=1, tiled=True)


def solution(mesh):
    return jax.shard_map(
        local,
        mesh=mesh,
        in_specs=(
            P("patch", "mode", None),
            P("patch", "mode"),
            P("patch", "mode", None, None),
            P("patch", "mode", None),
            P("mode", "patch"),
            P(),
            P("patch", "mode", None, None),
        ),
        out_specs=P(None, ("patch", "mode")),
        check_vma=False,
    )
```

profile of v0, /device:TPU:1, one launch (start us, length us, event | category | flops | bytes accessed | tf_op | source)
XLA Modules:
  0.0 323.2 jit_solution(18082024190553527620)
XLA Ops:
  6.5 0.8 convert_bitcast_fusion
  7.3 2.5 fusion.12
  9.8 0.0 all-gather.2.cloned.1.call-update
  9.8 0.0 reduce-scatter.2.cloned.1.call-start
  9.9 2.6 copy.20
  12.4 48.7 %sine_convert_fusion.6 = bf16[384,8192]{1,0:T(8,128)(2,1)} fusion(s32[384]{0:T(512)S(1)} %iota_add_fusion), kind=kLoop, calls=%fused_computation.6.clone.clone.clone.clone.1 | loop fusion | flops 47185920 | bytes 6292992 | tf_op jit(solution)/shard_map/dot_general | solution.py:20
  61.2 48.4 %cosine_convert_fusion.4 = bf16[384,8192]{1,0:T(8,128)(2,1)} fusion(s32[384]{0:T(512)S(1)} %iota_add_fusion), kind=kLoop, calls=%fused_computation.7.clone.clone.1 | loop fusion | flops 47185920 | bytes 6292992 | tf_op jit(solution)/shard_map/dot_general | solution.py:19
  109.6 8.0 %fusion.13 = f32[384,512]{1,0:T(8,128)S(1)} fusion(bf16[8192,512]{0,1:T(8,128)(2,1)} %all-gather.2.cloned.1.call-done, bf16[384,8192]{1,0:T(8,128)(2,1)} %sine_convert_fusion.6), kind=kOutput, calls=%fused_computation.19 | convolution fusion | flops 3221422080 | bytes 15466496 | tf_op jit(solution)/shard_map/dot_general | solution.py:20
  117.5 1.5 copy-done.4
  119.0 3.4 %fusion.6 = f32[384,512]{1,0:T(8,128)S(1)} fusion(bf16[8192,512]{0,1:T(8,128)(2,1)S(1)} %copy-done.4, bf16[384,8192]{1,0:T(8,128)(2,1)S(1)} %copy-done.1), kind=kOutput, calls=%fused_computation.11 | convolution fusion | flops 3221225472 | bytes 15466496 | tf_op jit(solution)/shard_map/dot_general | solution.py:19
  122.4 0.1 pad_maximum_fusion
  122.6 0.0 copy-start.3
  122.6 1.6 copy.15
  124.2 3.3 %copy.16 = f32[384,2,8,64]{3,2,1,0:T(8,128)} copy(f32[384,2,8,64]{0,3,2,1:T(8,128)} %bitcast.36) | data formatting | bytes 3145728 | tf_op jit(solution)/shard_map/reshape | solution.py:45
  127.5 5.3 %fusion.10 = bf16[8,384,2,64]{3,0,2,1:T(8,128)(2,1)S(1)} fusion(f32[384,2,8,64]{3,2,1,0:T(8,128)} %copy.16, f32[8,384,8,1]{0,2,3,1:T(8,128)} %copy.20), kind=kOutput, calls=%fused_computation.15 | convolution fusion | flops 38141952 | bytes 2457600 | tf_op jit(solution)/shard_map/rmk,mtrc->kmtc/dot_general | solution.py:47
  132.8 1.9 copy.18
  134.7 0.0 reduce-scatter.2.cloned.1.call-update
  134.7 0.0 all-reduce.3.cloned.1.call-start
  134.8 31.9 %reduce-scatter.2.cloned.1.call-done = bf16[1,384,2,64]{1,3,2,0:T(8,128)(2,1)} async-done(((bf16[8,384,2,64]{1,3,2,0:T(8,128)(2,1)}), bf16[1,384,2,64]{1,3,2,0:T(8,128)(2,1)}) %reduce-scatter.2.cloned.1.call-update) | async-done | bytes 98320 | tf_op jit(solution)/shard_map/reduce_scatter | solution.py:46
  166.7 1.1 fusion.14
  167.9 1.2 convolution_bitcast_fusion.1
  169.0 0.0 all-reduce.3.cloned.1.call-update
  169.0 146.4 %all-reduce.3.cloned.1.call-done = f32[64,512]{0,1:T(8,128)} async-done(((f32[64,512]{0,1:T(8,128)}), f32[64,512]{0,1:T(8,128)}) %all-reduce.3.cloned.1.call-update) | async-done | bytes 131088
  315.4 1.3 constant_dynamic-slice_fusion
  (12 shorter events, 0.0 us)
Async XLA Ops:
  6.5 161.3 %copy-start = (bf16[1,384,2,512]{3,2,1,0:T(2,128)(2,1)S(1)}, bf16[1,384,2,512]{3,2,1,0:T(2,128)(2,1)}, u32[]{:S(2)}) copy-start(bf16[1,384,2,512]{3,2,1,0:T(2,128)(2,1)} %param.13) | copy-start | bytes 2359300
  6.5 103.0 %all-gather.2.cloned.1.call-start = ((), (), s32[]{:S(2)}) async-start(), calls=%async_computation.1 | async-start | bytes 8912896 | tf_op jit(solution)/shard_map/all_gather | solution.py:42
  9.8 156.9 %reduce-scatter.2.cloned.1.call-start = ((), (), s32[]{:S(2)}) async-start(), calls=%async_computation.2 | async-start | bytes 884736 | tf_op jit(solution)/shard_map/reduce_scatter | solution.py:46
  109.6 8.0 %copy-start.1 = (bf16[384,8192]{1,0:T(8,128)(2,1)S(1)}, bf16[384,8192]{1,0:T(8,128)(2,1)}, u32[]{:S(2)}) copy-start(bf16[384,8192]{1,0:T(8,128)(2,1)} %cosine_convert_fusion.4) | copy-start | bytes 18874372
  109.6 9.4 %copy-start.4 = (bf16[8192,512]{0,1:T(8,128)(2,1)S(1)}, bf16[8192,512]{0,1:T(8,128)(2,1)}, u32[]{:S(2)}) copy-start(bf16[8192,512]{0,1:T(8,128)(2,1)} %all-gather.2.cloned.1.call-done) | copy-start | bytes 25165828
  122.6 12.2 %copy-start.3 = (f32[384,1]{0,1:T(1,128)S(1)}, f32[384,1]{0,1:T(1,128)}, u32[]{:S(2)}) copy-start(f32[384,1]{0,1:T(1,128)} %param.11) | copy-start | bytes 4612
  122.6 44.1 %copy-start.2 = (f32[64,64]{1,0:T(8,128)S(1)}, f32[64,64]{1,0:T(8,128)}, u32[]{:S(2)}) copy-start(f32[64,64]{1,0:T(8,128)} %param.12) | copy-start | bytes 49156
  134.7 180.7 %all-reduce.3.cloned.1.call-start = ((), (), s32[]{:S(2)}) async-start(), calls=%async_computation.3 | async-start | bytes 524288
Sparse Core Ops, SparseCore 0:
  9.9 80.7 all-gather.1
  134.8 31.8 reduce-scatter.1
  172.2 143.1 all-reduce.2
where the time goes:
time: 323 us
  waiting for transfers between devices  178 us (55%)
  other arithmetic  98.1 us (30%)
  matrix products  21.4 us (7%)
  between operations  13.2 us (4%)
  local copies, waits for them, and re-layouts  12.1 us (4%)
    unnamed x4, waiting for transfers between devices  146 us
    dot_general x1, other arithmetic, fourier(): imag_part = -jnp.dot(sine, values, preferred_element_type=jnp.float32)  48.7 us
    dot_general x1, other arithmetic, fourier(): real_part = jnp.dot(cosine, values, preferred_element_type=jnp.float32)  48.4 us
    reduce_scatter x1, waiting for transfers between devices, local(): lax.psum_scatter(jnp.einsum('rmk,mtrc->kmtc', cycle_legendre, four, preci...  31.9 us
    dot_general x1, matrix products, fourier(): imag_part = -jnp.dot(sine, values, preferred_element_type=jnp.float32)  7.95 us
  transfers between devices with their start and end apart: 3, of which 2 were waited for; matrix products, arithmetic and copies ran while one was open for 31% of the time, Pallas kernels for 0%

commit v1 on v0

v1 whole, which is shorter than its diff:
```python
import functools
import math

import jax
import jax.numpy as jnp
import numpy as np
from jax import lax
from jax.experimental import pallas as pl
from jax.experimental.pallas import tpu as pltpu
from jax.sharding import PartitionSpec as P

F32 = jnp.float32
BF16 = jnp.bfloat16
MESH = pl.DeviceIdType.MESH
NM = 16
NP = 8


def fourier_tables():
    m1 = np.arange(64)[:, None]
    j1 = np.arange(64)[None, :]
    angle = 2.0 * math.pi * ((m1 * j1) % 64) / 64.0
    wa = np.concatenate([np.cos(angle), -np.sin(angle)], axis=0)
    low = np.arange(128)[:, None]
    j2 = np.arange(128)[None, :]
    turn = 2.0 * math.pi * (low * j2) / 8192.0
    wb = np.zeros((48, 2, 4, 4, 2, 64))
    g = np.arange(48)[:, None]
    fold = np.arange(64)[None, :]
    phi = 2.0 * math.pi * ((g * fold) % 64) / 64.0
    for dd in range(4):
        wb[:, 0, dd, dd, 0, :] = np.cos(phi)
        wb[:, 0, dd, dd, 1, :] = np.sin(phi)
        wb[:, 1, dd, dd, 0, :] = -np.sin(phi)
        wb[:, 1, dd, dd, 1, :] = np.cos(phi)
    return (
        jnp.asarray(wa.astype(np.float32), BF16),
        jnp.asarray(wb.reshape(384, 512).astype(np.float32), BF16),
        jnp.asarray(np.cos(turn), F32),
        jnp.asarray(np.sin(turn), F32),
    )


def iota2(shape, axis):
    return lax.broadcasted_iota(jnp.int32, shape, axis)


def onehot(test):
    return jnp.where(test, 1.0, 0.0).astype(BF16)


def dot(a, b):
    return jnp.dot(a, b, preferred_element_type=F32)


def dot_nt(a, b):
    return lax.dot_general(a, b, (((1,), (1,)), ((), ())), preferred_element_type=F32)


def kernel(
    sky_h, mask_h, noise_h, leg_h, band_h, cov_h, test_h, wa_h, wb_h, twc_h, tws_h,
    out,
    sky, mask, noise, leg, band, cov, test, wa, wb, twc, tws,
    bd, xsend, xrecv, xs, lown, lall, lf, four, alm_a, alm_b, pair, zsend, zrecv,
    total, asend, arecv, tt, ce, fsend, frecv, gsend, grecv,
    in_sem, xs_sem, xr_sem, ls_sem, lr_sem, ps_sem, pr_sem, zs_sem, zr_sem,
    as_sem, ar_sem, fs_sem, fr_sem, gs_sem, gr_sem,
):
    p = lax.axis_index("patch")
    e = lax.axis_index("mode")
    core = lax.rem(p, 2)
    z = p // 2

    barrier = pltpu.get_barrier_semaphore()
    for i in range(1, NM):
        pl.semaphore_signal(barrier, inc=1, device_id=(p, lax.rem(e + i, NM)), device_id_type=MESH)
    for i in range(1, NP):
        pl.semaphore_signal(barrier, inc=1, device_id=(lax.rem(p + i, NP), e), device_id_type=MESH)

    hbm = (noise_h, sky_h, mask_h, leg_h, wa_h, twc_h, tws_h, wb_h, cov_h, band_h, test_h)
    vmem = (noise, sky, mask, leg, wa, twc, tws, wb, cov, band, test)
    loads = [pltpu.make_async_copy(a, b, in_sem.at[i]) for i, (a, b) in enumerate(zip(hbm, vmem))]
    for load in loads:
        load.start()

    row = iota2((512, 512), 0)
    lane = iota2((512, 512), 1)
    source = ((row >> 2) & 7) * 64 + (row >> 5) * 4 + (row & 3)
    order = onehot(lane == source)
    repeat = onehot((iota2((64, 512), 1) & 63) == iota2((64, 512), 0))
    loads[0].wait()
    moved = dot(order, noise[...].astype(BF16)).astype(BF16)
    wide = dot(moved, repeat)
    bd[...] = jnp.where((lane >> 6) == ((row >> 2) & 7), wide, 0.0).astype(BF16)
    loads[1].wait()
    loads[2].wait()
    for r in range(8):
        seen = jnp.broadcast_to(mask[r : r + 1, :].astype(F32), (64, 512)).astype(BF16)
        sky[64 * r : 64 * r + 64, :] = sky[64 * r : 64 * r + 64, :] * seen

    loads[3].wait()
    for t in range(3):
        lown[t] = leg[:, 128 * t : 128 * t + 128].astype(BF16)

    def send_x(i):
        to = lax.rem(e + i, NM)
        return pltpu.make_async_remote_copy(
            src_ref=xsend.at[to], dst_ref=xrecv.at[e], send_sem=xs_sem.at[i], recv_sem=xr_sem.at[e],
            device_id=(p, to), device_id_type=MESH)

    def send_l(i):
        to = lax.rem(e + i, NM)
        return pltpu.make_async_remote_copy(
            src_ref=lown, dst_ref=lall.at[e], send_sem=ls_sem.at[i], recv_sem=lr_sem.at[e],
            device_id=(p, to), device_id_type=MESH)

    for q in range(4):
        white = dot(bd[128 * q : 128 * q + 128, :], sky[...]).astype(BF16)
        xsend[4 * q : 4 * q + 4] = white.reshape(4, 32, 512)

    pl.semaphore_wait(barrier, NM - 1 + NP - 1)
    for i in range(1, NM):
        send_x(i).start()
    for i in range(1, NM):
        send_l(i).start()

    loads[10].wait()
    loads[8].wait()
    split = onehot(iota2((256, 256), 1) == 2 * (iota2((256, 256), 0) & 127) + (iota2((256, 256), 0) >> 7))
    s_to = iota2((512, 512), 1)
    s_from = ((s_to >> 2) & 7) * 64 + (s_to >> 5) * 4 + (s_to & 3)
    columns = onehot(iota2((512, 512), 0) == s_from)
    for b in range(3):
        block = test[128 * b : 128 * b + 128].reshape(256, 512)
        parts = dot(dot(split, block).astype(BF16), columns).astype(BF16)
        tt[128 * b : 128 * b + 128, :] = parts[:128]
        tt[384 + 128 * b : 384 + 128 * b + 128, :] = parts[128:]
    l128 = iota2((64, 128), 1)
    spread = onehot(iota2((64, 128), 0) == 4 * (l128 >> 3) + (l128 & 3))
    high = cov[...].astype(BF16)
    rest = (cov[...] - high.astype(F32)).astype(BF16)
    for n, piece in enumerate((high, rest)):
        wide_cov = dot(piece, spread)
        for t in range(2):
            ce[n, 64 * t : 64 * t + 64, :] = jnp.where(((l128 >> 2) & 1) == t, wide_cov, 0.0).astype(BF16)

    xrecv[e] = xsend[e]
    lall[e] = lown[...]

    def wait_x(src):
        pltpu.make_async_remote_copy(
            src_ref=xrecv.at[src], dst_ref=xrecv.at[src], send_sem=xs_sem.at[0], recv_sem=xr_sem.at[src],
            device_id=(p, e), device_id_type=MESH).wait_recv()

    def wait_l(src):
        pltpu.make_async_remote_copy(
            src_ref=lall.at[src], dst_ref=lall.at[src], send_sem=ls_sem.at[0], recv_sem=lr_sem.at[src],
            device_id=(p, e), device_id_type=MESH).wait_recv()

    def spread_x(src):
        for h in range(4):
            xs[pl.ds(src * 4 + h, 32, stride=64), :] = xrecv[src, :, 128 * h : 128 * h + 128].astype(F32)

    def spread_l(src):
        lf[pl.ds(pl.multiple_of(src * 192, 64), 192), :] = lall[src].reshape(192, 128).astype(F32)

    spread_x(e)
    spread_l(e)

    def take_x(i, carry):
        src = lax.rem(e + NM - i, NM)
        wait_x(src)
        spread_x(src)
        return carry

    lax.fori_loop(1, NM, take_x, 0)

    loads[4].wait()
    loads[5].wait()
    loads[6].wait()
    loads[7].wait()
    left_half = iota2((64, 128), 1) < 64

    def transform(pair_index, carry):
        rows = []
        for s in range(2):
            base = pair_index * 512 + s * 256
            pix = [xs[pl.ds(pl.multiple_of(base + 64 * dd, 64), 64), :] for dd in range(4)]
            first = dot(wa[...], jnp.concatenate(pix, axis=1).astype(BF16))
            lanes = []
            for dd in range(4):
                re = first[:64, 128 * dd : 128 * dd + 128]
                im = first[64:, 128 * dd : 128 * dd + 128]
                halves = []
                for h in range(2):
                    c = twc[64 * h : 64 * h + 64, :]
                    sn = tws[64 * h : 64 * h + 64, :]
                    tr = re * c + im * sn
                    ti = im * c - re * sn
                    halves.append(
                        jnp.where(left_half, tr, ti) + pltpu.roll(jnp.where(left_half, ti, tr), 64, 1))
                lanes.append(jnp.concatenate(halves, axis=0).astype(BF16))
            rows.append(jnp.concatenate(lanes, axis=1))
        second = dot_nt(wb[...], jnp.concatenate(rows, axis=0))
        four[2 * pair_index] = second[:, :128]
        four[2 * pair_index + 1] = second[:, 128:]
        return carry

    lax.fori_loop(0, 4, transform, 0)

    def take_l(i, carry):
        src = lax.rem(e + NM - i, NM)
        wait_l(src)
        spread_l(src)
        return carry

    lax.fori_loop(1, NM, take_l, 0)

    def legendre(parity, put):
        def body(gp, carry):
            acc = [[None, None] for _ in range(4)]
            for gi in range(2):
                g = 2 * gp + gi
                for r in range(8):
                    f = four[r, pl.ds(pl.multiple_of(g * 8, 8), 8), :]
                    for kk in range(4):
                        lrow = lf[pl.ds(g * 64 + r * 8 + 2 * kk + parity, 8, stride=0), :]
                        term = lrow * f
                        acc[kk][gi] = term if r == 0 else acc[kk][gi] + term
            for kk in range(4):
                put(kk, pl.ds(pl.multiple_of(gp * 16, 16), 16), jnp.concatenate(acc[kk], axis=0))
            return carry

        lax.fori_loop(0, 24, body, 0)

    def put_a(kk, rows, value):
        alm_a[kk, rows, :] = value.astype(BF16)

    def put_b(kk, rows, value):
        alm_b[kk, rows, :] = value

    legendre(1 - core, put_a)
    to_core = pltpu.make_async_remote_copy(
        src_ref=alm_a, dst_ref=pair, send_sem=ps_sem, recv_sem=pr_sem,
        device_id=(2 * z + 1 - core, e), device_id_type=MESH)
    to_core.start()
    legendre(core, put_b)
    to_core.wait_recv()
    z_copies = []
    for i in (2, 1, 3):
        kk = lax.rem(z + i, 4)
        zsend[i - 1] = (alm_b[kk] + pair[kk].astype(F32)).astype(BF16)
        copy = pltpu.make_async_remote_copy(
            src_ref=zsend.at[i - 1], dst_ref=zrecv.at[i - 1],
            send_sem=zs_sem.at[i - 1], recv_sem=zr_sem.at[i - 1],
            device_id=(2 * kk + core, e), device_id_type=MESH)
        copy.start()
        z_copies.append(copy)
    total[...] = alm_b[z] + pair[z].astype(F32)
    for copy in z_copies:
        copy.wait_recv()
    summed = total[...] + zrecv[0].astype(F32) + zrecv[1].astype(F32) + zrecv[2].astype(F32)

    for d in range(NM):
        asend[d, 0:24, :] = summed[24 * d : 24 * d + 24, :].astype(BF16)
        asend[d, 24:32, :] = jnp.zeros((8, 128), BF16)
    a_copies = []
    for i in range(1, NM):
        to = lax.rem(e + i, NM)
        copy = pltpu.make_async_remote_copy(
            src_ref=asend.at[to], dst_ref=arecv.at[e], send_sem=as_sem.at[i], recv_sem=ar_sem.at[e],
            device_id=(p, to), device_id_type=MESH)
        copy.start()
        a_copies.append(copy)
    arecv[e] = asend[e]
    for i in range(1, NM):
        src = lax.rem(e + NM - i, NM)
        pltpu.make_async_remote_copy(
            src_ref=arecv.at[src], dst_ref=arecv.at[src], send_sem=as_sem.at[0], recv_sem=ar_sem.at[src],
            device_id=(p, e), device_id_type=MESH).wait_recv()
    loads[9].wait()
    parts = arecv[...].astype(F32)
    alm = jnp.concatenate(
        [parts[:, 8 * gl : 8 * gl + 8, :].reshape(128, 128) for gl in range(3)], axis=1).astype(BF16)
    mixed = dot(ce[0], alm) + dot(ce[1], alm)
    scaled = (mixed * band[...]).astype(BF16)
    sketch = dot(scaled[:64], tt[:384, :]) + dot(scaled[64:], tt[384:, :])

    chunk = iota2((16, 128), 1) >> 5
    for tile in range(4):
        piece = [sketch[16 * q : 16 * q + 16, 128 * tile : 128 * tile + 128] for q in range(4)]
        for s in range(4):
            message = jnp.zeros((16, 128), F32)
            for q in range(4):
                shift = (32 * (q - s)) % 128
                moved_piece = piece[q] if shift == 0 else pltpu.roll(piece[q], shift, 1)
                message = jnp.where(chunk == q, moved_piece, message)
            fsend[4 * tile + s] = message
    f_copies = []
    for i in range(1, NM):
        to = lax.rem(e + i, NM)
        copy = pltpu.make_async_remote_copy(
            src_ref=fsend.at[to], dst_ref=frecv.at[e], send_sem=fs_sem.at[i], recv_sem=fr_sem.at[e],
            device_id=(p, to), device_id_type=MESH)
        copy.start()
        f_copies.append(copy)
    frecv[e] = fsend[e]
    for i in range(1, NM):
        src = lax.rem(e + NM - i, NM)
        pltpu.make_async_remote_copy(
            src_ref=frecv.at[src], dst_ref=frecv.at[src], send_sem=fs_sem.at[0], recv_sem=fr_sem.at[src],
            device_id=(p, e), device_id_type=MESH).wait_recv()
    gsend[...] = jnp.sum(frecv[...], axis=0)
    g_copies = []
    for i in range(1, NP):
        to = lax.rem(p + i, NP)
        copy = pltpu.make_async_remote_copy(
            src_ref=gsend, dst_ref=grecv.at[p], send_sem=gs_sem.at[i], recv_sem=gr_sem.at[p],
            device_id=(to, e), device_id_type=MESH)
        copy.start()
        g_copies.append(copy)
    grecv[p] = gsend[...]
    for i in range(1, NP):
        src = lax.rem(p + NP - i, NP)
        pltpu.make_async_remote_copy(
            src_ref=grecv.at[src], dst_ref=grecv.at[src], send_sem=gs_sem.at[0], recv_sem=gr_sem.at[src],
            device_id=(p, e), device_id_type=MESH).wait_recv()
    whole = jnp.sum(grecv[...], axis=0)
    for q in range(4):
        turned = pltpu.roll(whole, lax.rem(256 - 32 * q - 4 * p, 128), 1)
        out[16 * q : 16 * q + 16, :] = turned[:, :4]

    for i in range(1, NM):
        send_x(i).wait_send()
        send_l(i).wait_send()
    to_core.wait_send()
    for copy in z_copies + a_copies + f_copies + g_copies:
        copy.wait_send()


def local(sky_map, pixel_mask, noise_factor, cycle_legendre, band_power, channel_cov, test_matrix):
    wa, wb, twc, tws = fourier_tables()
    args = (
        jnp.transpose(sky_map, (0, 2, 1)).reshape(512, 512),
        pixel_mask,
        noise_factor.reshape(512, 64),
        jnp.transpose(cycle_legendre, (0, 2, 1)).reshape(64, 384),
        jnp.transpose(band_power),
        channel_cov,
        test_matrix.reshape(384, 2, 512),
        wa, wb, twc, tws,
    )
    dma = pltpu.SemaphoreType.DMA
    return pl.pallas_call(
        kernel,
        out_shape=jax.ShapeDtypeStruct((64, 4), F32),
        in_specs=[pl.BlockSpec(memory_space=pl.ANY)] * len(args),
        out_specs=pl.BlockSpec(memory_space=pltpu.VMEM),
        scratch_shapes=[
            pltpu.VMEM((512, 512), BF16),
            pltpu.VMEM((8, 512), jnp.int32),
            pltpu.VMEM((512, 64), F32),
            pltpu.VMEM((64, 384), F32),
            pltpu.VMEM((1, 384), F32),
            pltpu.VMEM((64, 64), F32),
            pltpu.VMEM((384, 2, 512), BF16),
            pltpu.VMEM((128, 64), BF16),
            pltpu.VMEM((384, 512), BF16),
            pltpu.VMEM((128, 128), F32),
            pltpu.VMEM((128, 128), F32),
            pltpu.VMEM((512, 512), BF16),
            pltpu.VMEM((16, 32, 512), BF16),
            pltpu.VMEM((16, 32, 512), BF16),
            pltpu.VMEM((2048, 128), F32),
            pltpu.VMEM((3, 64, 128), BF16),
            pltpu.VMEM((16, 3, 64, 128), BF16),
            pltpu.VMEM((3072, 128), F32),
            pltpu.VMEM((8, 384, 128), F32),
            pltpu.VMEM((4, 384, 128), BF16),
            pltpu.VMEM((4, 384, 128), F32),
            pltpu.VMEM((4, 384, 128), BF16),
            pltpu.VMEM((3, 384, 128), BF16),
            pltpu.VMEM((3, 384, 128), BF16),
            pltpu.VMEM((384, 128), F32),
            pltpu.VMEM((16, 32, 128), BF16),
            pltpu.VMEM((16, 32, 128), BF16),
            pltpu.VMEM((768, 512), BF16),
            pltpu.VMEM((2, 128, 128), BF16),
            pltpu.VMEM((16, 16, 128), F32),
            pltpu.VMEM((16, 16, 128), F32),
            pltpu.VMEM((16, 128), F32),
            pltpu.VMEM((8, 16, 128), F32),
            dma((11,)),
            dma((16,)), dma((16,)), dma((16,)), dma((16,)),
            dma, dma, dma((3,)), dma((3,)),
            dma((16,)), dma((16,)), dma((16,)), dma((16,)), dma((8,)), dma((8,)),
        ],
        compiler_params=pltpu.CompilerParams(collective_id=0, has_side_effects=True),
        name="harmonic_sketch",
    )(*args)


def solution(mesh):
    return jax.shard_map(
        local,
        mesh=mesh,
        in_specs=(
            P("patch", "mode", None),
            P("patch", "mode"),
            P("patch", "mode", None, None),
            P("patch", "mode", None),
            P("mode", "patch"),
            P(),
            P("patch", "mode", None, None),
        ),
        out_specs=P(None, ("patch", "mode")),
        check_vma=False,
    )
```

time: 323 us -> 53.8 us (0.17)
  waiting for transfers between devices: 178 us -> 0 us
  other arithmetic: 98.1 us -> 0 us
  Pallas kernels: 0 us -> 52.2 us
  matrix products: 21.4 us -> 0 us
  between operations: 13.2 us -> 0.01 us
  local copies, waits for them, and re-layouts: 12.1 us -> 1.41 us
    unnamed x4 -> x0, waiting for transfers between devices: 146 us -> none
    dot_general x2 -> x0, other arithmetic: 97.1 us -> none  [the longest x1 48.7 us: fourier(): imag_part = -jnp.dot(sine, values, preferred_element_type=jnp.float32)]
    pallas_call x0 -> x1, Pallas kernels: none -> 52.2 us  [local(): pl.pallas_call(kernel, out_shape=jax.ShapeDtypeStruct((64, 4), F32), in_s...]
    reduce_scatter x1 -> x0, waiting for transfers between devices: 31.9 us -> none  [local(): lax.psum_scatter(jnp.einsum('rmk,mtrc->kmtc', cycle_legendre, four, preci...]
    dot_general x6 -> x0, matrix products: 21.4 us -> none  [the longest x1 7.95 us: fourier(): imag_part = -jnp.dot(sine, values, preferred_element_type=jnp.float32)]
    unnamed x12 -> x0, local copies, waits for them, and re-layouts: 5.3 us -> none
    reshape x1 -> x0, local copies, waits for them, and re-layouts: 3.3 us -> none  [local(): four = four.reshape(mode_count, 2, cycle_count, chans)]
  transfers between devices with their start and end apart: 3 -> 0, of which waited for: 2 -> 0; matrix products, arithmetic and copies ran while one was open for 31% -> 0% of each run, Pallas kernels for 0% -> 0%
where the time goes in v1:
time: 53.8 us; the launch traced here: 53.6 us
  Pallas kernels  52.2 us (97%)
  local copies, waits for them, and re-layouts  1.41 us (3%)
    pallas_call x1, Pallas kernels, local(): pl.pallas_call(kernel, out_shape=jax.ShapeDtypeStruct((64, 4), F32), in_s...  52.2 us
    pallas_call x1, local copies, waits for them, and re-layouts, local(): pl.pallas_call(kernel, out_shape=jax.ShapeDtypeStruct((64, 4), F32), in_s...  1.41 us

profile of v1, /device:TPU:1, one launch (start us, length us, event | category | flops | bytes accessed | tf_op | source)
XLA Modules:
  0.0 53.6 jit_solution(10128973214488544120)
XLA Ops:
  0.0 52.2 %harmonic_sketch.1 = f32[64,4]{1,0:T(8,128)} custom-call(bf16[512,512]{1,0:T(8,128)(2,1)} %bitcast.10, s32[8,512]{1,0:T(8,128)} %mask_h.1, f32[512,64]{1,0:T(8,128)} %bitcast.11, f32[64,384]{1,0:T(8,128)} %bitcast.12, f32[1,384]{1,0:T(1,128)} %bitcast.13, f32[64,64]{1,0:T(8,128)} %cov_h.1, bf16[384,2,512]{2,1,0:T(2,128)(2,1)} %bitcast.9, ...), custom_call_target="tpu_custom_call" | custom-call | tf_op jit(solution)/shard_map/harmonic_sketch/pallas_call | solution.py:354
  52.2 1.4 %copy.12 = f32[64,4]{0,1:T(4,128)} copy(f32[64,4]{1,0:T(8,128)} %harmonic_sketch.1) | data formatting | bytes 2048 | tf_op jit(solution)/shard_map/harmonic_sketch/pallas_call | solution.py:354

commit v2 on v1

--- a/solution.py
+++ b/solution.py
@@ -62,14 +62,22 @@
     out,
     sky, mask, noise, leg, band, cov, test, wa, wb, twc, tws,
     bd, xsend, xrecv, xs, lown, lall, lf, four, alm_a, alm_b, pair, zsend, zrecv,
-    total, asend, arecv, tt, ce, fsend, frecv, gsend, grecv,
-    in_sem, xs_sem, xr_sem, ls_sem, lr_sem, ps_sem, pr_sem, zs_sem, zr_sem,
+    total, asend, arecv, tt, ce, fsend, frecv, gsend, grecv, turned,
+    in_sem, xs_sem, xr_sem, ls_sem, lf_sem, lr_sem, ps_sem, pr_sem, zs_sem, zr_sem,
     as_sem, ar_sem, fs_sem, fr_sem, gs_sem, gr_sem,
 ):
     p = lax.axis_index("patch")
     e = lax.axis_index("mode")
     core = lax.rem(p, 2)
     z = p // 2
+    ex = e // 4
+    ey = lax.rem(e, 4)
+
+    def ahead(a, b):
+        return lax.rem(ex + a, 4) * 4 + lax.rem(ey + b, 4)
+
+    def behind(a, b):
+        return lax.rem(ex + 4 - a, 4) * 4 + lax.rem(ey + 4 - b, 4)
 
     barrier = pltpu.get_barrier_semaphore()
     for i in range(1, NM):
@@ -99,30 +107,41 @@
         sky[64 * r : 64 * r + 64, :] = sky[64 * r : 64 * r + 64, :] * seen
 
     loads[3].wait()
-    for t in range(3):
-        lown[t] = leg[:, 128 * t : 128 * t + 128].astype(BF16)
-
-    def send_x(i):
-        to = lax.rem(e + i, NM)
-        return pltpu.make_async_remote_copy(
-            src_ref=xsend.at[to], dst_ref=xrecv.at[e], send_sem=xs_sem.at[i], recv_sem=xr_sem.at[e],
+    for h in range(2):
+        for t in range(3):
+            lown[h, t] = leg[32 * h : 32 * h + 32, 128 * t : 128 * t + 128].astype(BF16)
+
+    def send_x(a, b):
+        to = ahead(a, b)
+        return pltpu.make_async_remote_copy(
+            src_ref=xsend.at[to], dst_ref=xrecv.at[e], send_sem=xs_sem.at[4 * a + b], recv_sem=xr_sem.at[e],
             device_id=(p, to), device_id_type=MESH)
 
-    def send_l(i):
-        to = lax.rem(e + i, NM)
-        return pltpu.make_async_remote_copy(
-            src_ref=lown, dst_ref=lall.at[e], send_sem=ls_sem.at[i], recv_sem=lr_sem.at[e],
+    def send_l(a, b):
+        return pltpu.make_async_remote_copy(
+            src_ref=lown, dst_ref=lall.at[4 * a + b], send_sem=ls_sem.at[a, b], recv_sem=lr_sem.at[4 * a + b, 0],
+            device_id=(p, ahead(a, b)), device_id_type=MESH)
+
+    def relay_l(a, b, h):
+        source, to = ((4 * a, ahead(0, b)), (b, ahead(a, 0)))[h]
+        return pltpu.make_async_remote_copy(
+            src_ref=lall.at[source, h], dst_ref=lall.at[4 * a + b, h],
+            send_sem=lf_sem.at[4 * a + b, h], recv_sem=lr_sem.at[4 * a + b, h],
             device_id=(p, to), device_id_type=MESH)
 
-    for q in range(4):
-        white = dot(bd[128 * q : 128 * q + 128, :], sky[...]).astype(BF16)
-        xsend[4 * q : 4 * q + 4] = white.reshape(4, 32, 512)
+    straight = [(0, 2), (2, 0), (0, 1), (0, 3), (1, 0), (3, 0)]
+    relayed = [(a, b) for a in range(1, 4) for b in range(1, 4)]
 
     pl.semaphore_wait(barrier, NM - 1 + NP - 1)
-    for i in range(1, NM):
-        send_x(i).start()
-    for i in range(1, NM):
-        send_l(i).start()
+    for a, b in straight:
+        send_l(a, b).start()
+    for n in range(4):
+        q = lax.rem(ex + n, 4)
+        white = dot(bd[pl.ds(pl.multiple_of(128 * q, 128), 128), :], sky[...]).astype(BF16)
+        xsend[pl.ds(4 * q, 4)] = white.reshape(4, 32, 512)
+        for b in range(4):
+            if n + b > 0:
+                send_x(n, b).start()
 
     loads[10].wait()
     loads[8].wait()
@@ -144,33 +163,43 @@
         for t in range(2):
             ce[n, 64 * t : 64 * t + 64, :] = jnp.where(((l128 >> 2) & 1) == t, wide_cov, 0.0).astype(BF16)
 
-    xrecv[e] = xsend[e]
-    lall[e] = lown[...]
-
     def wait_x(src):
         pltpu.make_async_remote_copy(
             src_ref=xrecv.at[src], dst_ref=xrecv.at[src], send_sem=xs_sem.at[0], recv_sem=xr_sem.at[src],
             device_id=(p, e), device_id_type=MESH).wait_recv()
 
-    def wait_l(src):
+    def wait_l(slot, h=None):
+        ref = lall.at[slot] if h is None else lall.at[slot, h]
         pltpu.make_async_remote_copy(
-            src_ref=lall.at[src], dst_ref=lall.at[src], send_sem=ls_sem.at[0], recv_sem=lr_sem.at[src],
+            src_ref=ref, dst_ref=ref, send_sem=lf_sem.at[0, 0], recv_sem=lr_sem.at[slot, 0 if h is None else h],
             device_id=(p, e), device_id_type=MESH).wait_recv()
 
-    def spread_x(src):
+    def spread_x(ref, src):
         for h in range(4):
-            xs[pl.ds(src * 4 + h, 32, stride=64), :] = xrecv[src, :, 128 * h : 128 * h + 128].astype(F32)
-
-    def spread_l(src):
-        lf[pl.ds(pl.multiple_of(src * 192, 64), 192), :] = lall[src].reshape(192, 128).astype(F32)
-
-    spread_x(e)
-    spread_l(e)
+            xs[pl.ds(src * 4 + h, 32, stride=64), :] = ref[src, :, 128 * h : 128 * h + 128].astype(F32)
+
+    def spread_l(ref, slot):
+        for h in range(2):
+            for t in range(3):
+                lf[192 * slot + 64 * t + 32 * h : 192 * slot + 64 * t + 32 * h + 32, :] = ref[h, t].astype(F32)
+
+    for n in (1, 3, 2):
+        wait_l(4 * n)
+        for b in (2, 1, 3):
+            relay_l(n, b, 0).start()
+        wait_l(n)
+        for a in (2, 1, 3):
+            relay_l(a, n, 1).start()
+
+    spread_x(xsend, e)
+    spread_l(lown, 0)
+    for a, b in straight:
+        spread_l(lall.at[4 * a + b], 4 * a + b)
 
     def take_x(i, carry):
         src = lax.rem(e + NM - i, NM)
         wait_x(src)
-        spread_x(src)
+        spread_x(xrecv, src)
         return carry
 
     lax.fori_loop(1, NM, take_x, 0)
@@ -208,75 +237,90 @@
 
     lax.fori_loop(0, 4, transform, 0)
 
-    def take_l(i, carry):
-        src = lax.rem(e + NM - i, NM)
-        wait_l(src)
-        spread_l(src)
-        return carry
-
-    lax.fori_loop(1, NM, take_l, 0)
-
-    def legendre(parity, put):
-        def body(gp, carry):
+    def legendre(a, parity, put):
+        def body(j, carry):
             acc = [[None, None] for _ in range(4)]
             for gi in range(2):
-                g = 2 * gp + gi
+                q = 2 * j + gi
+                b = q // 3
+                g = 3 * (lax.rem(ex + 4 - a, 4) * 4 + lax.rem(ey + 4 - b, 4)) + q - 3 * b
                 for r in range(8):
                     f = four[r, pl.ds(pl.multiple_of(g * 8, 8), 8), :]
                     for kk in range(4):
-                        lrow = lf[pl.ds(g * 64 + r * 8 + 2 * kk + parity, 8, stride=0), :]
+                        lrow = lf[pl.ds((12 * a + q) * 64 + r * 8 + 2 * kk + parity, 8, stride=0), :]
                         term = lrow * f
                         acc[kk][gi] = term if r == 0 else acc[kk][gi] + term
             for kk in range(4):
-                put(kk, pl.ds(pl.multiple_of(gp * 16, 16), 16), jnp.concatenate(acc[kk], axis=0))
+                put(kk, pl.ds(pl.multiple_of(j * 16, 16), 16), jnp.concatenate(acc[kk], axis=0))
             return carry
 
-        lax.fori_loop(0, 24, body, 0)
-
-    def put_a(kk, rows, value):
-        alm_a[kk, rows, :] = value.astype(BF16)
-
-    def put_b(kk, rows, value):
-        alm_b[kk, rows, :] = value
-
-    legendre(1 - core, put_a)
-    to_core = pltpu.make_async_remote_copy(
-        src_ref=alm_a, dst_ref=pair, send_sem=ps_sem, recv_sem=pr_sem,
-        device_id=(2 * z + 1 - core, e), device_id_type=MESH)
-    to_core.start()
-    legendre(core, put_b)
-    to_core.wait_recv()
-    z_copies = []
-    for i in (2, 1, 3):
-        kk = lax.rem(z + i, 4)
-        zsend[i - 1] = (alm_b[kk] + pair[kk].astype(F32)).astype(BF16)
-        copy = pltpu.make_async_remote_copy(
-            src_ref=zsend.at[i - 1], dst_ref=zrecv.at[i - 1],
-            send_sem=zs_sem.at[i - 1], recv_sem=zr_sem.at[i - 1],
-            device_id=(2 * kk + core, e), device_id_type=MESH)
-        copy.start()
-        z_copies.append(copy)
-    total[...] = alm_b[z] + pair[z].astype(F32)
-    for copy in z_copies:
-        copy.wait_recv()
-    summed = total[...] + zrecv[0].astype(F32) + zrecv[1].astype(F32) + zrecv[2].astype(F32)
-
-    for d in range(NM):
-        asend[d, 0:24, :] = summed[24 * d : 24 * d + 24, :].astype(BF16)
-        asend[d, 24:32, :] = jnp.zeros((8, 128), BF16)
-    a_copies = []
-    for i in range(1, NM):
-        to = lax.rem(e + i, NM)
-        copy = pltpu.make_async_remote_copy(
-            src_ref=asend.at[to], dst_ref=arecv.at[e], send_sem=as_sem.at[i], recv_sem=ar_sem.at[e],
-            device_id=(p, to), device_id_type=MESH)
-        copy.start()
-        a_copies.append(copy)
-    arecv[e] = asend[e]
+        lax.fori_loop(0, 6, body, 0)
+
+    def to_core(n):
+        return pltpu.make_async_remote_copy(
+            src_ref=alm_a.at[n], dst_ref=pair.at[n], send_sem=ps_sem.at[n], recv_sem=pr_sem.at[n],
+            device_id=(2 * z + 1 - core, e), device_id_type=MESH)
+
+    def to_chip(n, i):
+        return pltpu.make_async_remote_copy(
+            src_ref=zsend.at[n, i - 1], dst_ref=zrecv.at[n, i - 1],
+            send_sem=zs_sem.at[n, i - 1], recv_sem=zr_sem.at[n, i - 1],
+            device_id=(2 * lax.rem(z + i, 4) + core, e), device_id_type=MESH)
+
+    def to_owner(n, b):
+        return pltpu.make_async_remote_copy(
+            src_ref=asend.at[n, b], dst_ref=arecv.at[e], send_sem=as_sem.at[n, b], recv_sem=ar_sem.at[e],
+            device_id=(p, behind(n, b)), device_id_type=MESH)
+
+    def group_terms(n):
+        for b in range(4):
+            if n > 0 and b > 0:
+                for h in range(2):
+                    wait_l(4 * n + b, h)
+                spread_l(lall.at[4 * n + b], 4 * n + b)
+
+        def put_a(kk, rows, value):
+            alm_a[n, kk, rows, :] = value.astype(BF16)
+
+        def put_b(kk, rows, value):
+            alm_b[n, kk, rows, :] = value
+
+        legendre(n, 1 - core, put_a)
+        to_core(n).start()
+        legendre(n, core, put_b)
+
+    def group_pair(n):
+        to_core(n).wait_recv()
+        for i in (2, 1, 3):
+            kk = lax.rem(z + i, 4)
+            zsend[n, i - 1] = (alm_b[n, kk] + pair[n, kk].astype(F32)).astype(BF16)
+            to_chip(n, i).start()
+        total[n] = alm_b[n, z] + pair[n, z].astype(F32)
+
+    def group_return(n):
+        for i in (1, 3, 2):
+            to_chip(n, i).wait_recv()
+        summed = total[n] + zrecv[n, 0].astype(F32) + zrecv[n, 1].astype(F32) + zrecv[n, 2].astype(F32)
+        for b in range(4):
+            asend[n, b, 0:24, :] = summed[24 * b : 24 * b + 24, :].astype(BF16)
+            asend[n, b, 24:32, :] = jnp.zeros((8, 128), BF16)
+            if n + b > 0:
+                to_owner(n, b).start()
+        if n == 0:
+            arecv[e] = asend[0, 0]
+
+    for n in range(6):
+        if n < 4:
+            group_terms(n)
+        if 1 <= n <= 4:
+            group_pair(n - 1)
+        if n >= 2:
+            group_return(n - 2)
+
     for i in range(1, NM):
         src = lax.rem(e + NM - i, NM)
         pltpu.make_async_remote_copy(
-            src_ref=arecv.at[src], dst_ref=arecv.at[src], send_sem=as_sem.at[0], recv_sem=ar_sem.at[src],
+            src_ref=arecv.at[src], dst_ref=arecv.at[src], send_sem=as_sem.at[0, 0], recv_sem=ar_sem.at[src],
             device_id=(p, e), device_id_type=MESH).wait_recv()
     loads[9].wait()
     parts = arecv[...].astype(F32)
@@ -326,15 +370,24 @@
             src_ref=grecv.at[src], dst_ref=grecv.at[src], send_sem=gs_sem.at[0], recv_sem=gr_sem.at[src],
             device_id=(p, e), device_id_type=MESH).wait_recv()
     whole = jnp.sum(grecv[...], axis=0)
-    for q in range(4):
-        turned = pltpu.roll(whole, lax.rem(256 - 32 * q - 4 * p, 128), 1)
-        out[16 * q : 16 * q + 16, :] = turned[:, :4]
-
-    for i in range(1, NM):
-        send_x(i).wait_send()
-        send_l(i).wait_send()
-    to_core.wait_send()
-    for copy in z_copies + a_copies + f_copies + g_copies:
+    turned[...] = jnp.transpose(whole)
+    out[...] = jnp.concatenate([turned[pl.ds(32 * q + 4 * p, 4), :] for q in range(4)], axis=1)
+
+    for a in range(4):
+        for b in range(4):
+            if a + b > 0:
+                send_x(a, b).wait_send()
+                to_owner(a, b).wait_send()
+    for a, b in straight:
+        send_l(a, b).wait_send()
+    for a, b in relayed:
+        for h in range(2):
+            relay_l(a, b, h).wait_send()
+    for n in range(4):
+        to_core(n).wait_send()
+        for i in range(1, 4):
+            to_chip(n, i).wait_send()
+    for copy in f_copies + g_copies:
         copy.wait_send()
 
 
@@ -351,9 +404,9 @@
         wa, wb, twc, tws,
     )
     dma = pltpu.SemaphoreType.DMA
-    return pl.pallas_call(
+    result = pl.pallas_call(
         kernel,
-        out_shape=jax.ShapeDtypeStruct((64, 4), F32),
+        out_shape=jax.ShapeDtypeStruct((4, 64), F32),
         in_specs=[pl.BlockSpec(memory_space=pl.ANY)] * len(args),
         out_specs=pl.BlockSpec(memory_space=pltpu.VMEM),
         scratch_shapes=[
@@ -372,17 +425,17 @@
             pltpu.VMEM((16, 32, 512), BF16),
             pltpu.VMEM((16, 32, 512), BF16),
             pltpu.VMEM((2048, 128), F32),
-            pltpu.VMEM((3, 64, 128), BF16),
-            pltpu.VMEM((16, 3, 64, 128), BF16),
+            pltpu.VMEM((2, 3, 32, 128), BF16),
+            pltpu.VMEM((16, 2, 3, 32, 128), BF16),
             pltpu.VMEM((3072, 128), F32),
             pltpu.VMEM((8, 384, 128), F32),
-            pltpu.VMEM((4, 384, 128), BF16),
-            pltpu.VMEM((4, 384, 128), F32),
-            pltpu.VMEM((4, 384, 128), BF16),
-            pltpu.VMEM((3, 384, 128), BF16),
-            pltpu.VMEM((3, 384, 128), BF16),
-            pltpu.VMEM((384, 128), F32),
-            pltpu.VMEM((16, 32, 128), BF16),
+            pltpu.VMEM((4, 4, 96, 128), BF16),
+            pltpu.VMEM((4, 4, 96, 128), F32),
+            pltpu.VMEM((4, 4, 96, 128), BF16),
+            pltpu.VMEM((4, 3, 96, 128), BF16),
+            pltpu.VMEM((4, 3, 96, 128), BF16),
+            pltpu.VMEM((4, 96, 128), F32),
+            pltpu.VMEM((4, 4, 32, 128), BF16),
             pltpu.VMEM((16, 32, 128), BF16),
             pltpu.VMEM((768, 512), BF16),
             pltpu.VMEM((2, 128, 128), BF16),
@@ -390,14 +443,16 @@
             pltpu.VMEM((16, 16, 128), F32),
             pltpu.VMEM((16, 128), F32),
             pltpu.VMEM((8, 16, 128), F32),
+            pltpu.VMEM((128, 16), F32),
             dma((11,)),
-            dma((16,)), dma((16,)), dma((16,)), dma((16,)),
-            dma, dma, dma((3,)), dma((3,)),
-            dma((16,)), dma((16,)), dma((16,)), dma((16,)), dma((8,)), dma((8,)),
+            dma((16,)), dma((16,)), dma((4, 4)), dma((16, 2)), dma((16, 2)),
+            dma((4,)), dma((4,)), dma((4, 3)), dma((4, 3)),
+            dma((4, 4)), dma((16,)), dma((16,)), dma((16,)), dma((8,)), dma((8,)),
         ],
         compiler_params=pltpu.CompilerParams(collective_id=0, has_side_effects=True),
         name="harmonic_sketch",
     )(*args)
+    return jnp.transpose(result)
 
 
 def solution(mesh):

time: 53.8 us -> 51.2 us (0.952)
  Pallas kernels: 52.2 us -> 49.8 us
    pallas_call x1, Pallas kernels: 52.2 us -> 49.8 us  [local(): pl.pallas_call(kernel, out_shape=jax.ShapeDtypeStruct((4, 64), F32), in_s...]
    pallas_call x1 -> x0, local copies, waits for them, and re-layouts: 1.41 us -> none  [local(): pl.pallas_call(kernel, out_shape=jax.ShapeDtypeStruct((64, 4), F32), in_s...]
    unnamed x0 -> x1, local copies, waits for them, and re-layouts: none -> 1.26 us
where the time goes in v2:
time: 51.2 us; the launch traced here: 51.1 us
  Pallas kernels  49.8 us (97%)
  local copies, waits for them, and re-layouts  1.26 us (2%)
    pallas_call x1, Pallas kernels, local(): pl.pallas_call(kernel, out_shape=jax.ShapeDtypeStruct((4, 64), F32), in_s...  49.8 us
    unnamed x1, local copies, waits for them, and re-layouts  1.26 us

profile of v2, /device:TPU:1, one launch (start us, length us, event | category | flops | bytes accessed | tf_op | source)
XLA Modules:
  0.0 51.1 jit_solution(11366038870888065470)
XLA Ops:
  0.0 49.8 %harmonic_sketch.1 = f32[4,64]{1,0:T(4,128)} custom-call(bf16[512,512]{1,0:T(8,128)(2,1)} %bitcast.11, s32[8,512]{1,0:T(8,128)} %mask_h.1, f32[512,64]{1,0:T(8,128)} %bitcast.12, f32[64,384]{1,0:T(8,128)} %bitcast.13, f32[1,384]{1,0:T(1,128)} %bitcast.15, f32[64,64]{1,0:T(8,128)} %cov_h.1, bf16[384,2,512]{2,1,0:T(2,128)(2,1)} %bitcast.10, ...), custom_call_target="tpu_custom_call" | custom-call | tf_op jit(solution)/shard_map/harmonic_sketch/pallas_call | solution.py:407
  49.8 1.3 %copy.13 = f32[64,4]{0,1:T(4,128)} copy(f32[64,4]{0,1:T(4,128)} %bitcast.14) | data formatting | bytes 2048

commit v3 on v2

--- a/solution.py
+++ b/solution.py
@@ -13,7 +13,7 @@
 BF16 = jnp.bfloat16
 MESH = pl.DeviceIdType.MESH
 NM = 16
-NP = 8
+RELAY_AT = 6
 
 
 def fourier_tables():
@@ -61,10 +61,10 @@
     sky_h, mask_h, noise_h, leg_h, band_h, cov_h, test_h, wa_h, wb_h, twc_h, tws_h,
     out,
     sky, mask, noise, leg, band, cov, test, wa, wb, twc, tws,
-    bd, xsend, xrecv, xs, lown, lall, lf, four, alm_a, alm_b, pair, zsend, zrecv,
-    total, asend, arecv, tt, ce, fsend, frecv, gsend, grecv, turned,
-    in_sem, xs_sem, xr_sem, ls_sem, lf_sem, lr_sem, ps_sem, pr_sem, zs_sem, zr_sem,
-    as_sem, ar_sem, fs_sem, fr_sem, gs_sem, gr_sem,
+    bd, xsend, xrecv, xs, lown, lall, lf, four, alm_a, alm_b, pair, asend, arecv, tt, ce,
+    ssend, srecv, fsend, frecv,
+    in_sem, xs_sem, xr_sem, ls_sem, lf_sem, lr_sem, ps_sem, pr_sem,
+    as_sem, ar_sem, ss_sem, sr_sem, fs_sem, fr_sem,
 ):
     p = lax.axis_index("patch")
     e = lax.axis_index("mode")
@@ -79,11 +79,16 @@
     def behind(a, b):
         return lax.rem(ex + 4 - a, 4) * 4 + lax.rem(ey + 4 - b, 4)
 
+    def plane(dz):
+        return 2 * lax.rem(z + dz, 4) + core
+
+    peers = [(dz, a, b) for dz in range(4) for a in range(4) for b in range(4) if dz + a + b > 0]
+    peers.sort(key=lambda t: -sum(min(v, 4 - v) for v in t))
+
     barrier = pltpu.get_barrier_semaphore()
-    for i in range(1, NM):
-        pl.semaphore_signal(barrier, inc=1, device_id=(p, lax.rem(e + i, NM)), device_id_type=MESH)
-    for i in range(1, NP):
-        pl.semaphore_signal(barrier, inc=1, device_id=(lax.rem(p + i, NP), e), device_id_type=MESH)
+    pl.semaphore_signal(barrier, inc=1, device_id=(2 * z + 1 - core, e), device_id_type=MESH)
+    for dz, a, b in peers:
+        pl.semaphore_signal(barrier, inc=1, device_id=(plane(dz), ahead(a, b)), device_id_type=MESH)
 
     hbm = (noise_h, sky_h, mask_h, leg_h, wa_h, twc_h, tws_h, wb_h, cov_h, band_h, test_h)
     vmem = (noise, sky, mask, leg, wa, twc, tws, wb, cov, band, test)
@@ -132,7 +137,7 @@
     straight = [(0, 2), (2, 0), (0, 1), (0, 3), (1, 0), (3, 0)]
     relayed = [(a, b) for a in range(1, 4) for b in range(1, 4)]
 
-    pl.semaphore_wait(barrier, NM - 1 + NP - 1)
+    pl.semaphore_wait(barrier, len(peers) + 1)
     for a, b in straight:
         send_l(a, b).start()
     for n in range(4):
@@ -146,14 +151,15 @@
     loads[10].wait()
     loads[8].wait()
     split = onehot(iota2((256, 256), 1) == 2 * (iota2((256, 256), 0) & 127) + (iota2((256, 256), 0) >> 7))
-    s_to = iota2((512, 512), 1)
-    s_from = ((s_to >> 2) & 7) * 64 + (s_to >> 5) * 4 + (s_to & 3)
-    columns = onehot(iota2((512, 512), 0) == s_from)
+    to = iota2((256, 512), 0)
+    wanted = ((to >> 5) & 3) * 128 + (to >> 7) * 64 + ((to >> 1) & 15) * 4 + (to & 1) * 2
+    columns = [onehot(iota2((256, 512), 1) == wanted + h) for h in range(2)]
     for b in range(3):
-        block = test[128 * b : 128 * b + 128].reshape(256, 512)
-        parts = dot(dot(split, block).astype(BF16), columns).astype(BF16)
-        tt[128 * b : 128 * b + 128, :] = parts[:128]
-        tt[384 + 128 * b : 384 + 128 * b + 128, :] = parts[128:]
+        block = dot(split, test[128 * b : 128 * b + 128].reshape(256, 512)).astype(BF16)
+        for h in range(2):
+            parts = dot_nt(columns[h], block).astype(BF16)
+            tt[h, :, 128 * b : 128 * b + 128] = parts[:, :128]
+            tt[h, :, 384 + 128 * b : 384 + 128 * b + 128] = parts[:, 128:]
     l128 = iota2((64, 128), 1)
     spread = onehot(iota2((64, 128), 0) == 4 * (l128 >> 3) + (l128 & 3))
     high = cov[...].astype(BF16)
@@ -183,6 +189,15 @@
             for t in range(3):
                 lf[192 * slot + 64 * t + 32 * h : 192 * slot + 64 * t + 32 * h + 32, :] = ref[h, t].astype(F32)
 
+    def take_x(i, carry):
+        src = lax.rem(e + NM - i, NM)
+        wait_x(src)
+        spread_x(xrecv, src)
+        return carry
+
+    spread_x(xsend, e)
+    spread_l(lown, 0)
+    lax.fori_loop(1, RELAY_AT, take_x, 0)
     for n in (1, 3, 2):
         wait_l(4 * n)
         for b in (2, 1, 3):
@@ -190,19 +205,9 @@
         wait_l(n)
         for a in (2, 1, 3):
             relay_l(a, n, 1).start()
-
-    spread_x(xsend, e)
-    spread_l(lown, 0)
+    lax.fori_loop(RELAY_AT, NM, take_x, 0)
     for a, b in straight:
         spread_l(lall.at[4 * a + b], 4 * a + b)
-
-    def take_x(i, carry):
-        src = lax.rem(e + NM - i, NM)
-        wait_x(src)
-        spread_x(xrecv, src)
-        return carry
-
-    lax.fori_loop(1, NM, take_x, 0)
 
     loads[4].wait()
     loads[5].wait()
@@ -261,16 +266,11 @@
             src_ref=alm_a.at[n], dst_ref=pair.at[n], send_sem=ps_sem.at[n], recv_sem=pr_sem.at[n],
             device_id=(2 * z + 1 - core, e), device_id_type=MESH)
 
-    def to_chip(n, i):
-        return pltpu.make_async_remote_copy(
-            src_ref=zsend.at[n, i - 1], dst_ref=zrecv.at[n, i - 1],
-            send_sem=zs_sem.at[n, i - 1], recv_sem=zr_sem.at[n, i - 1],
-            device_id=(2 * lax.rem(z + i, 4) + core, e), device_id_type=MESH)
-
-    def to_owner(n, b):
-        return pltpu.make_async_remote_copy(
-            src_ref=asend.at[n, b], dst_ref=arecv.at[e], send_sem=as_sem.at[n, b], recv_sem=ar_sem.at[e],
-            device_id=(p, behind(n, b)), device_id_type=MESH)
+    def to_owner(dz, n, b):
+        return pltpu.make_async_remote_copy(
+            src_ref=asend.at[n, dz, b], dst_ref=arecv.at[dz, e],
+            send_sem=as_sem.at[n, 4 * dz + b], recv_sem=ar_sem.at[dz, e],
+            device_id=(plane(dz), behind(n, b)), device_id_type=MESH)
 
     def group_terms(n):
         for b in range(4):
@@ -291,93 +291,64 @@
 
     def group_pair(n):
         to_core(n).wait_recv()
-        for i in (2, 1, 3):
-            kk = lax.rem(z + i, 4)
-            zsend[n, i - 1] = (alm_b[n, kk] + pair[n, kk].astype(F32)).astype(BF16)
-            to_chip(n, i).start()
-        total[n] = alm_b[n, z] + pair[n, z].astype(F32)
-
-    def group_return(n):
-        for i in (1, 3, 2):
-            to_chip(n, i).wait_recv()
-        summed = total[n] + zrecv[n, 0].astype(F32) + zrecv[n, 1].astype(F32) + zrecv[n, 2].astype(F32)
-        for b in range(4):
-            asend[n, b, 0:24, :] = summed[24 * b : 24 * b + 24, :].astype(BF16)
-            asend[n, b, 24:32, :] = jnp.zeros((8, 128), BF16)
-            if n + b > 0:
-                to_owner(n, b).start()
-        if n == 0:
-            arecv[e] = asend[0, 0]
-
-    for n in range(6):
+        for dz in (2, 1, 3, 0):
+            kk = lax.rem(z + dz, 4)
+            both = (alm_b[n, kk] + pair[n, kk].astype(F32)).astype(BF16)
+            for b in (2, 1, 3, 0):
+                asend[n, dz, b] = both[24 * b : 24 * b + 24, :]
+                if dz + n + b > 0:
+                    to_owner(dz, n, b).start()
+
+    for n in range(5):
         if n < 4:
             group_terms(n)
-        if 1 <= n <= 4:
+        if n > 0:
             group_pair(n - 1)
-        if n >= 2:
-            group_return(n - 2)
-
-    for i in range(1, NM):
-        src = lax.rem(e + NM - i, NM)
+    arecv[0, e] = asend[0, 0, 0]
+    for dz, a, b in reversed(peers):
+        ref = arecv.at[dz, behind(a, b)]
         pltpu.make_async_remote_copy(
-            src_ref=arecv.at[src], dst_ref=arecv.at[src], send_sem=as_sem.at[0, 0], recv_sem=ar_sem.at[src],
+            src_ref=ref, dst_ref=ref, send_sem=as_sem.at[0, 0], recv_sem=ar_sem.at[dz, behind(a, b)],
             device_id=(p, e), device_id_type=MESH).wait_recv()
     loads[9].wait()
-    parts = arecv[...].astype(F32)
+    parts = arecv[0].astype(F32) + arecv[1].astype(F32) + arecv[2].astype(F32) + arecv[3].astype(F32)
     alm = jnp.concatenate(
         [parts[:, 8 * gl : 8 * gl + 8, :].reshape(128, 128) for gl in range(3)], axis=1).astype(BF16)
     mixed = dot(ce[0], alm) + dot(ce[1], alm)
     scaled = (mixed * band[...]).astype(BF16)
-    sketch = dot(scaled[:64], tt[:384, :]) + dot(scaled[64:], tt[384:, :])
-
-    chunk = iota2((16, 128), 1) >> 5
-    for tile in range(4):
-        piece = [sketch[16 * q : 16 * q + 16, 128 * tile : 128 * tile + 128] for q in range(4)]
-        for s in range(4):
-            message = jnp.zeros((16, 128), F32)
-            for q in range(4):
-                shift = (32 * (q - s)) % 128
-                moved_piece = piece[q] if shift == 0 else pltpu.roll(piece[q], shift, 1)
-                message = jnp.where(chunk == q, moved_piece, message)
-            fsend[4 * tile + s] = message
-    f_copies = []
-    for i in range(1, NM):
-        to = lax.rem(e + i, NM)
-        copy = pltpu.make_async_remote_copy(
-            src_ref=fsend.at[to], dst_ref=frecv.at[e], send_sem=fs_sem.at[i], recv_sem=fr_sem.at[e],
-            device_id=(p, to), device_id_type=MESH)
-        copy.start()
-        f_copies.append(copy)
-    frecv[e] = fsend[e]
-    for i in range(1, NM):
-        src = lax.rem(e + NM - i, NM)
+    scaled = jnp.concatenate([scaled[:64], scaled[64:]], axis=1)
+    sketch = jnp.concatenate([dot_nt(tt[h], scaled) for h in range(2)], axis=1)
+    ssend[...] = sketch.reshape(2, 64, 2, 128)
+
+    to_sibling = pltpu.make_async_remote_copy(
+        src_ref=ssend.at[1 - core], dst_ref=srecv, send_sem=ss_sem, recv_sem=sr_sem,
+        device_id=(2 * z + 1 - core, e), device_id_type=MESH)
+    to_sibling.start()
+    to_sibling.wait_recv()
+    fsend[...] = ssend[core] + srecv[...]
+
+    def to_column(dz, a, b):
+        column = lax.rem(z + dz, 4) * 16 + ahead(a, b)
+        return pltpu.make_async_remote_copy(
+            src_ref=fsend.at[column], dst_ref=frecv.at[16 * z + e],
+            send_sem=fs_sem.at[16 * dz + 4 * a + b], recv_sem=fr_sem.at[16 * z + e],
+            device_id=(plane(dz), ahead(a, b)), device_id_type=MESH)
+
+    for dz, a, b in peers:
+        to_column(dz, a, b).start()
+    frecv[16 * z + e] = fsend[16 * z + e]
+    for dz, a, b in reversed(peers):
+        source = lax.rem(z + 4 - dz, 4) * 16 + behind(a, b)
+        ref = frecv.at[source]
         pltpu.make_async_remote_copy(
-            src_ref=frecv.at[src], dst_ref=frecv.at[src], send_sem=fs_sem.at[0], recv_sem=fr_sem.at[src],
+            src_ref=ref, dst_ref=ref, send_sem=fs_sem.at[0], recv_sem=fr_sem.at[source],
             device_id=(p, e), device_id_type=MESH).wait_recv()
-    gsend[...] = jnp.sum(frecv[...], axis=0)
-    g_copies = []
-    for i in range(1, NP):
-        to = lax.rem(p + i, NP)
-        copy = pltpu.make_async_remote_copy(
-            src_ref=gsend, dst_ref=grecv.at[p], send_sem=gs_sem.at[i], recv_sem=gr_sem.at[p],
-            device_id=(to, e), device_id_type=MESH)
-        copy.start()
-        g_copies.append(copy)
-    grecv[p] = gsend[...]
-    for i in range(1, NP):
-        src = lax.rem(p + NP - i, NP)
-        pltpu.make_async_remote_copy(
-            src_ref=grecv.at[src], dst_ref=grecv.at[src], send_sem=gs_sem.at[0], recv_sem=gr_sem.at[src],
-            device_id=(p, e), device_id_type=MESH).wait_recv()
-    whole = jnp.sum(grecv[...], axis=0)
-    turned[...] = jnp.transpose(whole)
-    out[...] = jnp.concatenate([turned[pl.ds(32 * q + 4 * p, 4), :] for q in range(4)], axis=1)
+    out[...] = jnp.sum(frecv[...], axis=0)
 
     for a in range(4):
         for b in range(4):
             if a + b > 0:
                 send_x(a, b).wait_send()
-                to_owner(a, b).wait_send()
     for a, b in straight:
         send_l(a, b).wait_send()
     for a, b in relayed:
@@ -385,10 +356,10 @@
             relay_l(a, b, h).wait_send()
     for n in range(4):
         to_core(n).wait_send()
-        for i in range(1, 4):
-            to_chip(n, i).wait_send()
-    for copy in f_copies + g_copies:
-        copy.wait_send()
+    for dz, a, b in peers:
+        to_owner(dz, a, b).wait_send()
+        to_column(dz, a, b).wait_send()
+    to_sibling.wait_send()
 
 
 def local(sky_map, pixel_mask, noise_factor, cycle_legendre, band_power, channel_cov, test_matrix):
@@ -406,7 +377,7 @@
     dma = pltpu.SemaphoreType.DMA
     result = pl.pallas_call(
         kernel,
-        out_shape=jax.ShapeDtypeStruct((4, 64), F32),
+        out_shape=jax.ShapeDtypeStruct((2, 128), F32),
         in_specs=[pl.BlockSpec(memory_space=pl.ANY)] * len(args),
         out_specs=pl.BlockSpec(memory_space=pltpu.VMEM),
         scratch_shapes=[
@@ -432,27 +403,22 @@
             pltpu.VMEM((4, 4, 96, 128), BF16),
             pltpu.VMEM((4, 4, 96, 128), F32),
             pltpu.VMEM((4, 4, 96, 128), BF16),
-            pltpu.VMEM((4, 3, 96, 128), BF16),
-            pltpu.VMEM((4, 3, 96, 128), BF16),
-            pltpu.VMEM((4, 96, 128), F32),
-            pltpu.VMEM((4, 4, 32, 128), BF16),
-            pltpu.VMEM((16, 32, 128), BF16),
-            pltpu.VMEM((768, 512), BF16),
+            pltpu.VMEM((4, 4, 4, 24, 128), BF16),
+            pltpu.VMEM((4, 16, 24, 128), BF16),
+            pltpu.VMEM((2, 256, 768), BF16),
             pltpu.VMEM((2, 128, 128), BF16),
-            pltpu.VMEM((16, 16, 128), F32),
-            pltpu.VMEM((16, 16, 128), F32),
-            pltpu.VMEM((16, 128), F32),
-            pltpu.VMEM((8, 16, 128), F32),
-            pltpu.VMEM((128, 16), F32),
+            pltpu.VMEM((2, 64, 2, 128), F32),
+            pltpu.VMEM((64, 2, 128), F32),
+            pltpu.VMEM((64, 2, 128), F32),
+            pltpu.VMEM((64, 2, 128), F32),
             dma((11,)),
             dma((16,)), dma((16,)), dma((4, 4)), dma((16, 2)), dma((16, 2)),
-            dma((4,)), dma((4,)), dma((4, 3)), dma((4, 3)),
-            dma((4, 4)), dma((16,)), dma((16,)), dma((16,)), dma((8,)), dma((8,)),
+            dma((4,)), dma((4,)), dma((4, 16)), dma((4, 16)), dma, dma, dma((64,)), dma((64,)),
         ],
         compiler_params=pltpu.CompilerParams(collective_id=0, has_side_effects=True),
         name="harmonic_sketch",
     )(*args)
-    return jnp.transpose(result)
+    return jnp.transpose(result.reshape(4, 64))
 
 
 def solution(mesh):

time: 51.2 us -> 47.5 us (0.928)
  Pallas kernels: 49.8 us -> 46 us
    pallas_call x1, Pallas kernels: 49.8 us -> 46 us  [local(): pl.pallas_call(kernel, out_shape=jax.ShapeDtypeStruct((2, 128), F32), in_...]
    reshape x0 -> x1, local copies, waits for them, and re-layouts: none -> 1.34 us  [local(): return jnp.transpose(result.reshape(4, 64))]
    unnamed x1 -> x0, local copies, waits for them, and re-layouts: 1.26 us -> none
where the time goes in v3:
time: 47.5 us; the launch traced here: 47.4 us
  Pallas kernels  46 us (97%)
  local copies, waits for them, and re-layouts  1.34 us (3%)
    pallas_call x1, Pallas kernels, local(): pl.pallas_call(kernel, out_shape=jax.ShapeDtypeStruct((2, 128), F32), in_...  46 us
    reshape x1, local copies, waits for them, and re-layouts, local(): return jnp.transpose(result.reshape(4, 64))  1.34 us

profile of v3, /device:TPU:1, one launch (start us, length us, event | category | flops | bytes accessed | tf_op | source)
XLA Modules:
  0.0 47.4 jit_solution(1695208496490236071)
XLA Ops:
  0.0 46.0 %harmonic_sketch.1 = f32[2,128]{1,0:T(2,128)} custom-call(bf16[512,512]{1,0:T(8,128)(2,1)} %bitcast.11, s32[8,512]{1,0:T(8,128)} %mask_h.1, f32[512,64]{1,0:T(8,128)} %bitcast.12, f32[64,384]{1,0:T(8,128)} %bitcast.13, f32[1,384]{1,0:T(1,128)} %bitcast.14, f32[64,64]{1,0:T(8,128)} %cov_h.1, bf16[384,2,512]{2,1,0:T(2,128)(2,1)} %bitcast.10, ...), custom_call_target="tpu_custom_call" | custom-call | tf_op jit(solution)/shard_map/harmonic_sketch/pallas_call | solution.py:378
  46.1 1.3 %reshape.19 = f32[4,64]{1,0:T(4,128)} reshape(f32[2,128]{1,0:T(2,128)} %harmonic_sketch.1) | data formatting | bytes 2048 | tf_op jit(solution)/shard_map/reshape | solution.py:421

commit v4 on v3

--- a/solution.py
+++ b/solution.py
@@ -13,7 +13,6 @@
 BF16 = jnp.bfloat16
 MESH = pl.DeviceIdType.MESH
 NM = 16
-RELAY_AT = 6
 
 
 def fourier_tables():
@@ -63,7 +62,7 @@
     sky, mask, noise, leg, band, cov, test, wa, wb, twc, tws,
     bd, xsend, xrecv, xs, lown, lall, lf, four, alm_a, alm_b, pair, asend, arecv, tt, ce,
     ssend, srecv, fsend, frecv,
-    in_sem, xs_sem, xr_sem, ls_sem, lf_sem, lr_sem, ps_sem, pr_sem,
+    in_sem, xs_sem, xr_sem, ls_sem, ld_sem, lf_sem, lr_sem, ps_sem, pr_sem,
     as_sem, ar_sem, ss_sem, sr_sem, fs_sem, fr_sem,
 ):
     p = lax.axis_index("patch")
@@ -87,7 +86,8 @@
 
     barrier = pltpu.get_barrier_semaphore()
     pl.semaphore_signal(barrier, inc=1, device_id=(2 * z + 1 - core, e), device_id_type=MESH)
-    for dz, a, b in peers:
+    greeted = [(dz, a, b) for dz, a, b in peers if dz == 0 or a + b == 0]
+    for dz, a, b in greeted:
         pl.semaphore_signal(barrier, inc=1, device_id=(plane(dz), ahead(a, b)), device_id_type=MESH)
 
     hbm = (noise_h, sky_h, mask_h, leg_h, wa_h, twc_h, tws_h, wb_h, cov_h, band_h, test_h)
@@ -119,25 +119,24 @@
     def send_x(a, b):
         to = ahead(a, b)
         return pltpu.make_async_remote_copy(
-            src_ref=xsend.at[to], dst_ref=xrecv.at[e], send_sem=xs_sem.at[4 * a + b], recv_sem=xr_sem.at[e],
+            src_ref=xsend.at[to], dst_ref=xrecv.at[e], send_sem=xs_sem, recv_sem=xr_sem,
             device_id=(p, to), device_id_type=MESH)
 
     def send_l(a, b):
         return pltpu.make_async_remote_copy(
-            src_ref=lown, dst_ref=lall.at[4 * a + b], send_sem=ls_sem.at[a, b], recv_sem=lr_sem.at[4 * a + b, 0],
+            src_ref=lown, dst_ref=lall.at[4 * a + b], send_sem=ls_sem, recv_sem=ld_sem.at[0 if a == 0 else 1],
             device_id=(p, ahead(a, b)), device_id_type=MESH)
 
     def relay_l(a, b, h):
         source, to = ((4 * a, ahead(0, b)), (b, ahead(a, 0)))[h]
         return pltpu.make_async_remote_copy(
             src_ref=lall.at[source, h], dst_ref=lall.at[4 * a + b, h],
-            send_sem=lf_sem.at[4 * a + b, h], recv_sem=lr_sem.at[4 * a + b, h],
+            send_sem=lf_sem, recv_sem=lr_sem.at[a],
             device_id=(p, to), device_id_type=MESH)
 
     straight = [(0, 2), (2, 0), (0, 1), (0, 3), (1, 0), (3, 0)]
-    relayed = [(a, b) for a in range(1, 4) for b in range(1, 4)]
-
-    pl.semaphore_wait(barrier, len(peers) + 1)
+
+    pl.semaphore_wait(barrier, len(greeted) + 1)
     for a, b in straight:
         send_l(a, b).start()
     for n in range(4):
@@ -169,16 +168,9 @@
         for t in range(2):
             ce[n, 64 * t : 64 * t + 64, :] = jnp.where(((l128 >> 2) & 1) == t, wide_cov, 0.0).astype(BF16)
 
-    def wait_x(src):
-        pltpu.make_async_remote_copy(
-            src_ref=xrecv.at[src], dst_ref=xrecv.at[src], send_sem=xs_sem.at[0], recv_sem=xr_sem.at[src],
-            device_id=(p, e), device_id_type=MESH).wait_recv()
-
-    def wait_l(slot, h=None):
-        ref = lall.at[slot] if h is None else lall.at[slot, h]
-        pltpu.make_async_remote_copy(
-            src_ref=ref, dst_ref=ref, send_sem=lf_sem.at[0, 0], recv_sem=lr_sem.at[slot, 0 if h is None else h],
-            device_id=(p, e), device_id_type=MESH).wait_recv()
+    def copied(ref, sem):
+        return pltpu.make_async_remote_copy(
+            src_ref=ref, dst_ref=ref, send_sem=sem, recv_sem=sem, device_id=(p, e), device_id_type=MESH)
 
     def spread_x(ref, src):
         for h in range(4):
@@ -189,23 +181,23 @@
             for t in range(3):
                 lf[192 * slot + 64 * t + 32 * h : 192 * slot + 64 * t + 32 * h + 32, :] = ref[h, t].astype(F32)
 
-    def take_x(i, carry):
-        src = lax.rem(e + NM - i, NM)
-        wait_x(src)
-        spread_x(xrecv, src)
-        return carry
-
     spread_x(xsend, e)
     spread_l(lown, 0)
-    lax.fori_loop(1, RELAY_AT, take_x, 0)
+    copied(lall.at[pl.ds(0, 3)], ld_sem.at[1]).wait_recv()
     for n in (1, 3, 2):
-        wait_l(4 * n)
         for b in (2, 1, 3):
             relay_l(n, b, 0).start()
-        wait_l(n)
+    copied(lall.at[pl.ds(0, 3)], ld_sem.at[0]).wait_recv()
+    for n in (1, 3, 2):
         for a in (2, 1, 3):
             relay_l(a, n, 1).start()
-    lax.fori_loop(RELAY_AT, NM, take_x, 0)
+    copied(xrecv.at[pl.ds(0, NM - 1)], xr_sem).wait_recv()
+
+    def take_x(i, carry):
+        spread_x(xrecv, lax.rem(e + i, NM))
+        return carry
+
+    lax.fori_loop(1, NM, take_x, 0)
     for a, b in straight:
         spread_l(lall.at[4 * a + b], 4 * a + b)
 
@@ -263,20 +255,19 @@
 
     def to_core(n):
         return pltpu.make_async_remote_copy(
-            src_ref=alm_a.at[n], dst_ref=pair.at[n], send_sem=ps_sem.at[n], recv_sem=pr_sem.at[n],
+            src_ref=alm_a.at[n], dst_ref=pair.at[n], send_sem=ps_sem, recv_sem=pr_sem.at[n],
             device_id=(2 * z + 1 - core, e), device_id_type=MESH)
 
     def to_owner(dz, n, b):
         return pltpu.make_async_remote_copy(
-            src_ref=asend.at[n, dz, b], dst_ref=arecv.at[dz, e],
-            send_sem=as_sem.at[n, 4 * dz + b], recv_sem=ar_sem.at[dz, e],
+            src_ref=asend.at[n, dz, b], dst_ref=arecv.at[16 * dz + e],
+            send_sem=as_sem, recv_sem=ar_sem,
             device_id=(plane(dz), behind(n, b)), device_id_type=MESH)
 
     def group_terms(n):
-        for b in range(4):
-            if n > 0 and b > 0:
-                for h in range(2):
-                    wait_l(4 * n + b, h)
+        if n > 0:
+            copied(lall.at[pl.ds(0, 3)], lr_sem.at[n]).wait_recv()
+            for b in range(1, 4):
                 spread_l(lall.at[4 * n + b], 4 * n + b)
 
         def put_a(kk, rows, value):
@@ -304,14 +295,10 @@
             group_terms(n)
         if n > 0:
             group_pair(n - 1)
-    arecv[0, e] = asend[0, 0, 0]
-    for dz, a, b in reversed(peers):
-        ref = arecv.at[dz, behind(a, b)]
-        pltpu.make_async_remote_copy(
-            src_ref=ref, dst_ref=ref, send_sem=as_sem.at[0, 0], recv_sem=ar_sem.at[dz, behind(a, b)],
-            device_id=(p, e), device_id_type=MESH).wait_recv()
+    arecv[e] = asend[0, 0, 0]
+    copied(arecv.at[pl.ds(0, 63)], ar_sem).wait_recv()
     loads[9].wait()
-    parts = arecv[0].astype(F32) + arecv[1].astype(F32) + arecv[2].astype(F32) + arecv[3].astype(F32)
+    parts = sum(arecv[16 * dz : 16 * dz + 16].astype(F32) for dz in range(4))
     alm = jnp.concatenate(
         [parts[:, 8 * gl : 8 * gl + 8, :].reshape(128, 128) for gl in range(3)], axis=1).astype(BF16)
     mixed = dot(ce[0], alm) + dot(ce[1], alm)
@@ -331,35 +318,22 @@
         column = lax.rem(z + dz, 4) * 16 + ahead(a, b)
         return pltpu.make_async_remote_copy(
             src_ref=fsend.at[column], dst_ref=frecv.at[16 * z + e],
-            send_sem=fs_sem.at[16 * dz + 4 * a + b], recv_sem=fr_sem.at[16 * z + e],
+            send_sem=fs_sem, recv_sem=fr_sem,
             device_id=(plane(dz), ahead(a, b)), device_id_type=MESH)
 
     for dz, a, b in peers:
         to_column(dz, a, b).start()
     frecv[16 * z + e] = fsend[16 * z + e]
-    for dz, a, b in reversed(peers):
-        source = lax.rem(z + 4 - dz, 4) * 16 + behind(a, b)
-        ref = frecv.at[source]
-        pltpu.make_async_remote_copy(
-            src_ref=ref, dst_ref=ref, send_sem=fs_sem.at[0], recv_sem=fr_sem.at[source],
-            device_id=(p, e), device_id_type=MESH).wait_recv()
+    copied(frecv.at[pl.ds(0, 63)], fr_sem).wait_recv()
     out[...] = jnp.sum(frecv[...], axis=0)
 
-    for a in range(4):
-        for b in range(4):
-            if a + b > 0:
-                send_x(a, b).wait_send()
-    for a, b in straight:
-        send_l(a, b).wait_send()
-    for a, b in relayed:
-        for h in range(2):
-            relay_l(a, b, h).wait_send()
-    for n in range(4):
-        to_core(n).wait_send()
-    for dz, a, b in peers:
-        to_owner(dz, a, b).wait_send()
-        to_column(dz, a, b).wait_send()
+    copied(xrecv.at[pl.ds(0, NM - 1)], xs_sem).wait_send()
+    copied(lall.at[pl.ds(0, 6)], ls_sem).wait_send()
+    copied(lall.at[pl.ds(0, 9)], lf_sem).wait_send()
+    copied(alm_a, ps_sem).wait_send()
+    copied(arecv.at[pl.ds(0, 63)], as_sem).wait_send()
     to_sibling.wait_send()
+    copied(frecv.at[pl.ds(0, 63)], fs_sem).wait_send()
 
 
 def local(sky_map, pixel_mask, noise_factor, cycle_legendre, band_power, channel_cov, test_matrix):
@@ -404,16 +378,15 @@
             pltpu.VMEM((4, 4, 96, 128), F32),
             pltpu.VMEM((4, 4, 96, 128), BF16),
             pltpu.VMEM((4, 4, 4, 24, 128), BF16),
-            pltpu.VMEM((4, 16, 24, 128), BF16),
+            pltpu.VMEM((64, 24, 128), BF16),
             pltpu.VMEM((2, 256, 768), BF16),
             pltpu.VMEM((2, 128, 128), BF16),
             pltpu.VMEM((2, 64, 2, 128), F32),
             pltpu.VMEM((64, 2, 128), F32),
             pltpu.VMEM((64, 2, 128), F32),
             pltpu.VMEM((64, 2, 128), F32),
-            dma((11,)),
-            dma((16,)), dma((16,)), dma((4, 4)), dma((16, 2)), dma((16, 2)),
-            dma((4,)), dma((4,)), dma((4, 16)), dma((4, 16)), dma, dma, dma((64,)), dma((64,)),
+            dma((11,)), dma, dma, dma, dma((2,)), dma, dma((4,)),
+            dma, dma((4,)), dma, dma, dma, dma, dma, dma,
         ],
         compiler_params=pltpu.CompilerParams(collective_id=0, has_side_effects=True),
         name="harmonic_sketch",

time: 47.5 us -> 43.5 us (0.916)
  Pallas kernels: 46 us -> 42 us
    pallas_call x1, Pallas kernels: 46 us -> 42 us  [local(): pl.pallas_call(kernel, out_shape=jax.ShapeDtypeStruct((2, 128), F32), in_...]
where the time goes in v4:
time: 43.5 us; the launch traced here: 43.3 us
  Pallas kernels  42 us (97%)
  local copies, waits for them, and re-layouts  1.34 us (3%)
    pallas_call x1, Pallas kernels, local(): pl.pallas_call(kernel, out_shape=jax.ShapeDtypeStruct((2, 128), F32), in_...  42 us
    reshape x1, local copies, waits for them, and re-layouts, local(): return jnp.transpose(result.reshape(4, 64))  1.34 us

profile of v4, /device:TPU:1, one launch (start us, length us, event | category | flops | bytes accessed | tf_op | source)
XLA Modules:
  0.0 43.3 jit_solution(14678859583464195668)
XLA Ops:
  0.0 42.0 %harmonic_sketch.1 = f32[2,128]{1,0:T(2,128)} custom-call(bf16[512,512]{1,0:T(8,128)(2,1)} %bitcast.11, s32[8,512]{1,0:T(8,128)} %mask_h.1, f32[512,64]{1,0:T(8,128)} %bitcast.12, f32[64,384]{1,0:T(8,128)} %bitcast.13, f32[1,384]{1,0:T(1,128)} %bitcast.14, f32[64,64]{1,0:T(8,128)} %cov_h.1, bf16[384,2,512]{2,1,0:T(2,128)(2,1)} %bitcast.10, ...), custom_call_target="tpu_custom_call" | custom-call | tf_op jit(solution)/shard_map/harmonic_sketch/pallas_call | solution.py:352
  42.0 1.3 %reshape.19 = f32[4,64]{1,0:T(4,128)} reshape(f32[2,128]{1,0:T(2,128)} %harmonic_sketch.1) | data formatting | bytes 2048 | tf_op jit(solution)/shard_map/reshape | solution.py:394

commit v5 on v4

--- a/solution.py
+++ b/solution.py
@@ -23,18 +23,16 @@
     low = np.arange(128)[:, None]
     j2 = np.arange(128)[None, :]
     turn = 2.0 * math.pi * (low * j2) / 8192.0
-    wb = np.zeros((48, 2, 4, 4, 2, 64))
     g = np.arange(48)[:, None]
-    fold = np.arange(64)[None, :]
-    phi = 2.0 * math.pi * ((g * fold) % 64) / 64.0
-    for dd in range(4):
-        wb[:, 0, dd, dd, 0, :] = np.cos(phi)
-        wb[:, 0, dd, dd, 1, :] = np.sin(phi)
-        wb[:, 1, dd, dd, 0, :] = -np.sin(phi)
-        wb[:, 1, dd, dd, 1, :] = np.cos(phi)
+    phi = 2.0 * math.pi * ((g * j2) % 64) / 64.0
+    wb = np.zeros((48, 2, 2, 128))
+    wb[:, 0, 0, :] = np.cos(phi)
+    wb[:, 0, 1, :] = np.sin(phi)
+    wb[:, 1, 0, :] = -np.sin(phi)
+    wb[:, 1, 1, :] = np.cos(phi)
     return (
         jnp.asarray(wa.astype(np.float32), BF16),
-        jnp.asarray(wb.reshape(384, 512).astype(np.float32), BF16),
+        jnp.asarray(wb.reshape(96, 256).astype(np.float32), BF16),
         jnp.asarray(np.cos(turn), F32),
         jnp.asarray(np.sin(turn), F32),
     )
@@ -60,7 +58,7 @@
     sky_h, mask_h, noise_h, leg_h, band_h, cov_h, test_h, wa_h, wb_h, twc_h, tws_h,
     out,
     sky, mask, noise, leg, band, cov, test, wa, wb, twc, tws,
-    bd, xsend, xrecv, xs, lown, lall, lf, four, alm_a, alm_b, pair, asend, arecv, tt, ce,
+    bd, xsend, xrecv, xs, fa, turned, lown, lall, lf, four, alm_a, alm_b, pair, asend, arecv, tt, ce,
     ssend, srecv, fsend, frecv,
     in_sem, xs_sem, xr_sem, ls_sem, ld_sem, lf_sem, lr_sem, ps_sem, pr_sem,
     as_sem, ar_sem, ss_sem, sr_sem, fs_sem, fr_sem,
@@ -116,10 +114,10 @@
         for t in range(3):
             lown[h, t] = leg[32 * h : 32 * h + 32, 128 * t : 128 * t + 128].astype(BF16)
 
-    def send_x(a, b):
+    def send_x(a, b, half):
         to = ahead(a, b)
         return pltpu.make_async_remote_copy(
-            src_ref=xsend.at[to], dst_ref=xrecv.at[e], send_sem=xs_sem, recv_sem=xr_sem,
+            src_ref=xsend.at[half, to], dst_ref=xrecv.at[half, e], send_sem=xs_sem, recv_sem=xr_sem.at[half],
             device_id=(p, to), device_id_type=MESH)
 
     def send_l(a, b):
@@ -142,10 +140,16 @@
     for n in range(4):
         q = lax.rem(ex + n, 4)
         white = dot(bd[pl.ds(pl.multiple_of(128 * q, 128), 128), :], sky[...]).astype(BF16)
-        xsend[pl.ds(4 * q, 4)] = white.reshape(4, 32, 512)
+        white = white.reshape(4, 32, 512)
+        for half in range(2):
+            xsend[half, pl.ds(4 * q, 4)] = white[:, 16 * half : 16 * half + 16, :]
         for b in range(4):
             if n + b > 0:
-                send_x(n, b).start()
+                send_x(n, b, 0).start()
+    for a in range(4):
+        for b in range(4):
+            if a + b > 0:
+                send_x(a, b, 1).start()
 
     loads[10].wait()
     loads[8].wait()
@@ -172,16 +176,18 @@
         return pltpu.make_async_remote_copy(
             src_ref=ref, dst_ref=ref, send_sem=sem, recv_sem=sem, device_id=(p, e), device_id_type=MESH)
 
-    def spread_x(ref, src):
+    def spread_x(ref, half, src):
         for h in range(4):
-            xs[pl.ds(src * 4 + h, 32, stride=64), :] = ref[src, :, 128 * h : 128 * h + 128].astype(F32)
+            xs[pl.ds(1024 * half + src * 4 + h, 16, stride=64), :] = (
+                ref[half, src, :, 128 * h : 128 * h + 128].astype(F32))
 
     def spread_l(ref, slot):
         for h in range(2):
             for t in range(3):
                 lf[192 * slot + 64 * t + 32 * h : 192 * slot + 64 * t + 32 * h + 32, :] = ref[h, t].astype(F32)
 
-    spread_x(xsend, e)
+    spread_x(xsend, 0, e)
+    spread_x(xsend, 1, e)
     spread_l(lown, 0)
     copied(lall.at[pl.ds(0, 3)], ld_sem.at[1]).wait_recv()
     for n in (1, 3, 2):
@@ -191,48 +197,42 @@
     for n in (1, 3, 2):
         for a in (2, 1, 3):
             relay_l(a, n, 1).start()
-    copied(xrecv.at[pl.ds(0, NM - 1)], xr_sem).wait_recv()
-
-    def take_x(i, carry):
-        spread_x(xrecv, lax.rem(e + i, NM))
-        return carry
-
-    lax.fori_loop(1, NM, take_x, 0)
     for a, b in straight:
         spread_l(lall.at[4 * a + b], 4 * a + b)
-
-    loads[4].wait()
-    loads[5].wait()
-    loads[6].wait()
-    loads[7].wait()
-    left_half = iota2((64, 128), 1) < 64
-
-    def transform(pair_index, carry):
-        rows = []
-        for s in range(2):
-            base = pair_index * 512 + s * 256
-            pix = [xs[pl.ds(pl.multiple_of(base + 64 * dd, 64), 64), :] for dd in range(4)]
-            first = dot(wa[...], jnp.concatenate(pix, axis=1).astype(BF16))
-            lanes = []
+    for n in (4, 5, 6, 7):
+        loads[n].wait()
+
+    def twiddle(r, carry):
+        for h in range(2):
+            c = twc[64 * h : 64 * h + 64, :]
+            sn = tws[64 * h : 64 * h + 64, :]
+            rows = pl.ds(pl.multiple_of(lax.rem(r, 2) * 128 + 64 * h, 64), 64)
             for dd in range(4):
-                re = first[:64, 128 * dd : 128 * dd + 128]
-                im = first[64:, 128 * dd : 128 * dd + 128]
-                halves = []
-                for h in range(2):
-                    c = twc[64 * h : 64 * h + 64, :]
-                    sn = tws[64 * h : 64 * h + 64, :]
-                    tr = re * c + im * sn
-                    ti = im * c - re * sn
-                    halves.append(
-                        jnp.where(left_half, tr, ti) + pltpu.roll(jnp.where(left_half, ti, tr), 64, 1))
-                lanes.append(jnp.concatenate(halves, axis=0).astype(BF16))
-            rows.append(jnp.concatenate(lanes, axis=1))
-        second = dot_nt(wb[...], jnp.concatenate(rows, axis=0))
-        four[2 * pair_index] = second[:, :128]
-        four[2 * pair_index + 1] = second[:, 128:]
+                cols = slice(128 * dd, 128 * dd + 128)
+                re = fa[pl.ds(pl.multiple_of(128 * r, 128), 64), cols]
+                im = fa[pl.ds(pl.multiple_of(128 * r + 64, 64), 64), cols]
+                unit = 4 * (r // 2) + dd
+                turned[unit, rows, 0:128] = (re * c + im * sn).astype(BF16)
+                turned[unit, rows, 128:256] = (im * c - re * sn).astype(BF16)
         return carry
 
-    lax.fori_loop(0, 4, transform, 0)
+    for half in range(2):
+        copied(xrecv.at[half, pl.ds(0, NM - 1)], xr_sem.at[half]).wait_recv()
+
+        def take_x(i, carry, half=half):
+            spread_x(xrecv, half, lax.rem(e + i, NM))
+            return carry
+
+        lax.fori_loop(1, NM, take_x, 0)
+        for r in range(4 * half, 4 * half + 4):
+            pix = jnp.concatenate([xs[256 * r + 64 * dd : 256 * r + 64 * dd + 64, :] for dd in range(4)], axis=1)
+            fa[128 * r : 128 * r + 128, :] = dot(wa[...], pix.astype(BF16))
+        lax.fori_loop(4 * half, 4 * half + 4, twiddle, 0)
+        for unit in range(8 * half, 8 * half + 8):
+            second = dot_nt(wb[...], turned[unit])
+            for s in range(2):
+                start = (2 * (unit // 4) + s) * 384 + unit % 4
+                four[pl.ds(start, 96, stride=4), :] = second[:, 128 * s : 128 * s + 128]
 
     def legendre(a, parity, put):
         def body(j, carry):
@@ -242,7 +242,7 @@
                 b = q // 3
                 g = 3 * (lax.rem(ex + 4 - a, 4) * 4 + lax.rem(ey + 4 - b, 4)) + q - 3 * b
                 for r in range(8):
-                    f = four[r, pl.ds(pl.multiple_of(g * 8, 8), 8), :]
+                    f = four[pl.ds(pl.multiple_of(r * 384 + g * 8, 8), 8), :]
                     for kk in range(4):
                         lrow = lf[pl.ds((12 * a + q) * 64 + r * 8 + 2 * kk + parity, 8, stride=0), :]
                         term = lrow * f
@@ -251,7 +251,7 @@
                 put(kk, pl.ds(pl.multiple_of(j * 16, 16), 16), jnp.concatenate(acc[kk], axis=0))
             return carry
 
-        lax.fori_loop(0, 6, body, 0)
+        lax.fori_loop(0, 6, body, 0, unroll=3)
 
     def to_core(n):
         return pltpu.make_async_remote_copy(
@@ -327,7 +327,7 @@
     copied(frecv.at[pl.ds(0, 63)], fr_sem).wait_recv()
     out[...] = jnp.sum(frecv[...], axis=0)
 
-    copied(xrecv.at[pl.ds(0, NM - 1)], xs_sem).wait_send()
+    copied(xrecv.at[:, pl.ds(0, NM - 1)], xs_sem).wait_send()
     copied(lall.at[pl.ds(0, 6)], ls_sem).wait_send()
     copied(lall.at[pl.ds(0, 9)], lf_sem).wait_send()
     copied(alm_a, ps_sem).wait_send()
@@ -363,17 +363,19 @@
             pltpu.VMEM((64, 64), F32),
             pltpu.VMEM((384, 2, 512), BF16),
             pltpu.VMEM((128, 64), BF16),
-            pltpu.VMEM((384, 512), BF16),
+            pltpu.VMEM((96, 256), BF16),
             pltpu.VMEM((128, 128), F32),
             pltpu.VMEM((128, 128), F32),
             pltpu.VMEM((512, 512), BF16),
-            pltpu.VMEM((16, 32, 512), BF16),
-            pltpu.VMEM((16, 32, 512), BF16),
+            pltpu.VMEM((2, 16, 16, 512), BF16),
+            pltpu.VMEM((2, 16, 16, 512), BF16),
             pltpu.VMEM((2048, 128), F32),
+            pltpu.VMEM((1024, 512), F32),
+            pltpu.VMEM((16, 256, 256), BF16),
             pltpu.VMEM((2, 3, 32, 128), BF16),
             pltpu.VMEM((16, 2, 3, 32, 128), BF16),
             pltpu.VMEM((3072, 128), F32),
-            pltpu.VMEM((8, 384, 128), F32),
+            pltpu.VMEM((3072, 128), F32),
             pltpu.VMEM((4, 4, 96, 128), BF16),
             pltpu.VMEM((4, 4, 96, 128), F32),
             pltpu.VMEM((4, 4, 96, 128), BF16),
@@ -385,7 +387,7 @@
             pltpu.VMEM((64, 2, 128), F32),
             pltpu.VMEM((64, 2, 128), F32),
             pltpu.VMEM((64, 2, 128), F32),
-            dma((11,)), dma, dma, dma, dma((2,)), dma, dma((4,)),
+            dma((11,)), dma, dma((2,)), dma, dma((2,)), dma, dma((4,)),
             dma, dma((4,)), dma, dma, dma, dma, dma, dma,
         ],
         compiler_params=pltpu.CompilerParams(collective_id=0, has_side_effects=True),

time: 43.5 us -> 41.2 us (0.947)
  Pallas kernels: 42 us -> 39.7 us
    pallas_call x1, Pallas kernels: 42 us -> 39.7 us  [local(): pl.pallas_call(kernel, out_shape=jax.ShapeDtypeStruct((2, 128), F32), in_...]
where the time goes in v5:
time: 41.2 us; the launch traced here: 41 us
  Pallas kernels  39.7 us (96%)
  local copies, waits for them, and re-layouts  1.34 us (3%)
    pallas_call x1, Pallas kernels, local(): pl.pallas_call(kernel, out_shape=jax.ShapeDtypeStruct((2, 128), F32), in_...  39.7 us
    reshape x1, local copies, waits for them, and re-layouts, local(): return jnp.transpose(result.reshape(4, 64))  1.34 us

profile of v5, /device:TPU:1, one launch (start us, length us, event | category | flops | bytes accessed | tf_op | source)
XLA Modules:
  0.0 41.0 jit_solution(17730345005177610884)
XLA Ops:
  0.0 39.7 %harmonic_sketch.1 = f32[2,128]{1,0:T(2,128)} custom-call(bf16[512,512]{1,0:T(8,128)(2,1)} %bitcast.11, s32[8,512]{1,0:T(8,128)} %mask_h.1, f32[512,64]{1,0:T(8,128)} %bitcast.12, f32[64,384]{1,0:T(8,128)} %bitcast.13, f32[1,384]{1,0:T(1,128)} %bitcast.14, f32[64,64]{1,0:T(8,128)} %cov_h.1, bf16[384,2,512]{2,1,0:T(2,128)(2,1)} %bitcast.10, ...), custom_call_target="tpu_custom_call" | custom-call | tf_op jit(solution)/shard_map/harmonic_sketch/pallas_call | solution.py:352
  39.7 1.3 %reshape.19 = f32[4,64]{1,0:T(4,128)} reshape(f32[2,128]{1,0:T(2,128)} %harmonic_sketch.1) | data formatting | bytes 2048 | tf_op jit(solution)/shard_map/reshape | solution.py:396

commit v6 on v5

--- a/solution.py
+++ b/solution.py
@@ -129,27 +129,27 @@
         source, to = ((4 * a, ahead(0, b)), (b, ahead(a, 0)))[h]
         return pltpu.make_async_remote_copy(
             src_ref=lall.at[source, h], dst_ref=lall.at[4 * a + b, h],
-            send_sem=lf_sem, recv_sem=lr_sem.at[a],
+            send_sem=lf_sem, recv_sem=lr_sem.at[(b - a) % 3],
             device_id=(p, to), device_id_type=MESH)
 
+    shifts = [(a, (a + n) % 4) for n in range(4) for a in range(4)]
+    order = [(0, 0), (0, 2), (0, 1), (0, 3), (2, 0), (1, 0), (3, 0)]
+    order += [(a, (a + n - 1) % 3 + 1) for n in range(3) for a in range(1, 4)]
+    groups = [(0, 4), (4, 7), (7, 10), (10, 13), (13, 16)]
     straight = [(0, 2), (2, 0), (0, 1), (0, 3), (1, 0), (3, 0)]
 
     pl.semaphore_wait(barrier, len(greeted) + 1)
-    for a, b in straight:
-        send_l(a, b).start()
-    for n in range(4):
-        q = lax.rem(ex + n, 4)
-        white = dot(bd[pl.ds(pl.multiple_of(128 * q, 128), 128), :], sky[...]).astype(BF16)
-        white = white.reshape(4, 32, 512)
+    for q in range(4):
+        white = dot(bd[128 * q : 128 * q + 128, :], sky[...]).astype(BF16).reshape(4, 32, 512)
         for half in range(2):
-            xsend[half, pl.ds(4 * q, 4)] = white[:, 16 * half : 16 * half + 16, :]
-        for b in range(4):
-            if n + b > 0:
-                send_x(n, b, 0).start()
-    for a in range(4):
-        for b in range(4):
+            xsend[half, 4 * q : 4 * q + 4] = white[:, 16 * half : 16 * half + 16, :]
+    for half in range(2):
+        for a, b in shifts:
             if a + b > 0:
-                send_x(a, b, 1).start()
+                send_x(a, b, half).start()
+        if half == 0:
+            for a, b in straight:
+                send_l(a, b).start()
 
     loads[10].wait()
     loads[8].wait()
@@ -181,24 +181,14 @@
             xs[pl.ds(1024 * half + src * 4 + h, 16, stride=64), :] = (
                 ref[half, src, :, 128 * h : 128 * h + 128].astype(F32))
 
-    def spread_l(ref, slot):
+    def spread_l(ref, place):
         for h in range(2):
             for t in range(3):
-                lf[192 * slot + 64 * t + 32 * h : 192 * slot + 64 * t + 32 * h + 32, :] = ref[h, t].astype(F32)
+                lf[192 * place + 64 * t + 32 * h : 192 * place + 64 * t + 32 * h + 32, :] = ref[h, t].astype(F32)
 
     spread_x(xsend, 0, e)
     spread_x(xsend, 1, e)
     spread_l(lown, 0)
-    copied(lall.at[pl.ds(0, 3)], ld_sem.at[1]).wait_recv()
-    for n in (1, 3, 2):
-        for b in (2, 1, 3):
-            relay_l(n, b, 0).start()
-    copied(lall.at[pl.ds(0, 3)], ld_sem.at[0]).wait_recv()
-    for n in (1, 3, 2):
-        for a in (2, 1, 3):
-            relay_l(a, n, 1).start()
-    for a, b in straight:
-        spread_l(lall.at[4 * a + b], 4 * a + b)
     for n in (4, 5, 6, 7):
         loads[n].wait()
 
@@ -233,69 +223,79 @@
             for s in range(2):
                 start = (2 * (unit // 4) + s) * 384 + unit % 4
                 four[pl.ds(start, 96, stride=4), :] = second[:, 128 * s : 128 * s + 128]
-
-    def legendre(a, parity, put):
-        def body(j, carry):
-            acc = [[None, None] for _ in range(4)]
-            for gi in range(2):
-                q = 2 * j + gi
-                b = q // 3
-                g = 3 * (lax.rem(ex + 4 - a, 4) * 4 + lax.rem(ey + 4 - b, 4)) + q - 3 * b
+        if half == 0:
+            copied(lall.at[pl.ds(0, 3)], ld_sem.at[1]).wait_recv()
+            copied(lall.at[pl.ds(0, 3)], ld_sem.at[0]).wait_recv()
+            for n in (1, 3, 2):
+                for m in (2, 1, 3):
+                    relay_l(n, m, 0).start()
+                    relay_l(m, n, 1).start()
+            for place in range(1, 7):
+                a, b = order[place]
+                spread_l(lall.at[4 * a + b], place)
+
+    def legendre(place, parity, put):
+        a, b = order[place]
+        owner = behind(a, b)
+        for kk0 in range(0, 4, 2):
+            acc = [[None] * 3 for _ in range(2)]
+            for gl in range(3):
                 for r in range(8):
-                    f = four[pl.ds(pl.multiple_of(r * 384 + g * 8, 8), 8), :]
-                    for kk in range(4):
-                        lrow = lf[pl.ds((12 * a + q) * 64 + r * 8 + 2 * kk + parity, 8, stride=0), :]
+                    f = four[pl.ds(pl.multiple_of(384 * r + 24 * owner + 8 * gl, 8), 8), :]
+                    for kk in range(2):
+                        lrow = lf[pl.ds(192 * place + 64 * gl + 8 * r + 2 * (kk0 + kk) + parity, 8, stride=0), :]
                         term = lrow * f
-                        acc[kk][gi] = term if r == 0 else acc[kk][gi] + term
-            for kk in range(4):
-                put(kk, pl.ds(pl.multiple_of(j * 16, 16), 16), jnp.concatenate(acc[kk], axis=0))
-            return carry
-
-        lax.fori_loop(0, 6, body, 0, unroll=3)
+                        acc[kk][gl] = term if r == 0 else acc[kk][gl] + term
+            for kk in range(2):
+                put(kk0 + kk, jnp.concatenate(acc[kk], axis=0))
 
     def to_core(n):
-        return pltpu.make_async_remote_copy(
-            src_ref=alm_a.at[n], dst_ref=pair.at[n], send_sem=ps_sem, recv_sem=pr_sem.at[n],
+        first, last = groups[n]
+        part = pl.ds(first, last - first)
+        return pltpu.make_async_remote_copy(
+            src_ref=alm_a.at[part], dst_ref=pair.at[part], send_sem=ps_sem, recv_sem=pr_sem.at[n],
             device_id=(2 * z + 1 - core, e), device_id_type=MESH)
 
-    def to_owner(dz, n, b):
-        return pltpu.make_async_remote_copy(
-            src_ref=asend.at[n, dz, b], dst_ref=arecv.at[16 * dz + e],
+    def to_owner(dz, place):
+        a, b = order[place]
+        return pltpu.make_async_remote_copy(
+            src_ref=asend.at[place, dz], dst_ref=arecv.at[16 * dz + e],
             send_sem=as_sem, recv_sem=ar_sem,
-            device_id=(plane(dz), behind(n, b)), device_id_type=MESH)
+            device_id=(plane(dz), behind(a, b)), device_id_type=MESH)
 
     def group_terms(n):
-        if n > 0:
-            copied(lall.at[pl.ds(0, 3)], lr_sem.at[n]).wait_recv()
-            for b in range(1, 4):
-                spread_l(lall.at[4 * n + b], 4 * n + b)
-
-        def put_a(kk, rows, value):
-            alm_a[n, kk, rows, :] = value.astype(BF16)
-
-        def put_b(kk, rows, value):
-            alm_b[n, kk, rows, :] = value
-
-        legendre(n, 1 - core, put_a)
+        if n >= 2:
+            copied(lall.at[pl.ds(0, 3)], lr_sem.at[n - 2]).wait_recv()
+            for place in range(*groups[n]):
+                a, b = order[place]
+                spread_l(lall.at[4 * a + b], place)
+
+        for place in range(*groups[n]):
+            def put_a(kk, value):
+                alm_a[place, kk] = value.astype(BF16)
+
+            legendre(place, 1 - core, put_a)
         to_core(n).start()
-        legendre(n, core, put_b)
+        for place in range(*groups[n]):
+            def put_b(kk, value):
+                alm_b[place, kk] = value
+
+            legendre(place, core, put_b)
 
     def group_pair(n):
         to_core(n).wait_recv()
         for dz in (2, 1, 3, 0):
             kk = lax.rem(z + dz, 4)
-            both = (alm_b[n, kk] + pair[n, kk].astype(F32)).astype(BF16)
-            for b in (2, 1, 3, 0):
-                asend[n, dz, b] = both[24 * b : 24 * b + 24, :]
-                if dz + n + b > 0:
-                    to_owner(dz, n, b).start()
-
-    for n in range(5):
-        if n < 4:
-            group_terms(n)
-        if n > 0:
-            group_pair(n - 1)
-    arecv[e] = asend[0, 0, 0]
+            for place in range(*groups[n]):
+                asend[place, dz] = (alm_b[place, kk] + pair[place, kk].astype(F32)).astype(BF16)
+                if dz + place > 0:
+                    to_owner(dz, place).start()
+
+    for n in range(len(groups)):
+        group_terms(n)
+    for n in range(len(groups)):
+        group_pair(n)
+    arecv[e] = asend[0, 0]
     copied(arecv.at[pl.ds(0, 63)], ar_sem).wait_recv()
     loads[9].wait()
     parts = sum(arecv[16 * dz : 16 * dz + 16].astype(F32) for dz in range(4))
@@ -376,10 +376,10 @@
             pltpu.VMEM((16, 2, 3, 32, 128), BF16),
             pltpu.VMEM((3072, 128), F32),
             pltpu.VMEM((3072, 128), F32),
-            pltpu.VMEM((4, 4, 96, 128), BF16),
-            pltpu.VMEM((4, 4, 96, 128), F32),
-            pltpu.VMEM((4, 4, 96, 128), BF16),
-            pltpu.VMEM((4, 4, 4, 24, 128), BF16),
+            pltpu.VMEM((16, 4, 24, 128), BF16),
+            pltpu.VMEM((16, 4, 24, 128), F32),
+            pltpu.VMEM((16, 4, 24, 128), BF16),
+            pltpu.VMEM((16, 4, 24, 128), BF16),
             pltpu.VMEM((64, 24, 128), BF16),
             pltpu.VMEM((2, 256, 768), BF16),
             pltpu.VMEM((2, 128, 128), BF16),
@@ -387,8 +387,8 @@
             pltpu.VMEM((64, 2, 128), F32),
             pltpu.VMEM((64, 2, 128), F32),
             pltpu.VMEM((64, 2, 128), F32),
-            dma((11,)), dma, dma((2,)), dma, dma((2,)), dma, dma((4,)),
-            dma, dma((4,)), dma, dma, dma, dma, dma, dma,
+            dma((11,)), dma, dma((2,)), dma, dma((2,)), dma, dma((3,)),
+            dma, dma((5,)), dma, dma, dma, dma, dma, dma,
         ],
         compiler_params=pltpu.CompilerParams(collective_id=0, has_side_effects=True),
         name="harmonic_sketch",

time: 41.2 us -> 41.5 us (level)
  no operation moved by 1% of the time
where the time goes in v6:
time: 41.5 us; the launch traced here: 41.4 us
  Pallas kernels  40 us (96%)
  local copies, waits for them, and re-layouts  1.34 us (3%)
    pallas_call x1, Pallas kernels, local(): pl.pallas_call(kernel, out_shape=jax.ShapeDtypeStruct((2, 128), F32), in_...  40 us
    reshape x1, local copies, waits for them, and re-layouts, local(): return jnp.transpose(result.reshape(4, 64))  1.34 us

profile of v6, /device:TPU:1, one launch (start us, length us, event | category | flops | bytes accessed | tf_op | source)
XLA Modules:
  0.0 41.4 jit_solution(6411676937840077952)
XLA Ops:
  0.0 40.0 %harmonic_sketch.1 = f32[2,128]{1,0:T(2,128)} custom-call(bf16[512,512]{1,0:T(8,128)(2,1)} %bitcast.11, s32[8,512]{1,0:T(8,128)} %mask_h.1, f32[512,64]{1,0:T(8,128)} %bitcast.12, f32[64,384]{1,0:T(8,128)} %bitcast.13, f32[1,384]{1,0:T(1,128)} %bitcast.14, f32[64,64]{1,0:T(8,128)} %cov_h.1, bf16[384,2,512]{2,1,0:T(2,128)(2,1)} %bitcast.10, ...), custom_call_target="tpu_custom_call" | custom-call | tf_op jit(solution)/shard_map/harmonic_sketch/pallas_call | solution.py:352
  40.0 1.3 %reshape.19 = f32[4,64]{1,0:T(4,128)} reshape(f32[2,128]{1,0:T(2,128)} %harmonic_sketch.1) | data formatting | bytes 2048 | tf_op jit(solution)/shard_map/reshape | solution.py:396

commit v7 on v5

--- a/solution.py
+++ b/solution.py
@@ -290,11 +290,10 @@
                 if dz + n + b > 0:
                     to_owner(dz, n, b).start()
 
-    for n in range(5):
-        if n < 4:
-            group_terms(n)
-        if n > 0:
-            group_pair(n - 1)
+    for n in range(4):
+        group_terms(n)
+    for n in range(4):
+        group_pair(n)
     arecv[e] = asend[0, 0, 0]
     copied(arecv.at[pl.ds(0, 63)], ar_sem).wait_recv()
     loads[9].wait()
@@ -369,13 +368,13 @@
             pltpu.VMEM((512, 512), BF16),
             pltpu.VMEM((2, 16, 16, 512), BF16),
             pltpu.VMEM((2, 16, 16, 512), BF16),
-            pltpu.VMEM((2048, 128), F32),
+            pltpu.VMEM((2112, 128), F32),
             pltpu.VMEM((1024, 512), F32),
             pltpu.VMEM((16, 256, 256), BF16),
             pltpu.VMEM((2, 3, 32, 128), BF16),
             pltpu.VMEM((16, 2, 3, 32, 128), BF16),
-            pltpu.VMEM((3072, 128), F32),
-            pltpu.VMEM((3072, 128), F32),
+            pltpu.VMEM((3080, 128), F32),
+            pltpu.VMEM((3080, 128), F32),
             pltpu.VMEM((4, 4, 96, 128), BF16),
             pltpu.VMEM((4, 4, 96, 128), F32),
             pltpu.VMEM((4, 4, 96, 128), BF16),

time: 41.2 us -> 41.2 us (level)
  no operation moved by 1% of the time
where the time goes in v7:
time: 41.2 us; the launch traced here: 41 us
  Pallas kernels  39.7 us (96%)
  local copies, waits for them, and re-layouts  1.34 us (3%)
    pallas_call x1, Pallas kernels, local(): pl.pallas_call(kernel, out_shape=jax.ShapeDtypeStruct((2, 128), F32), in_...  39.7 us
    reshape x1, local copies, waits for them, and re-layouts, local(): return jnp.transpose(result.reshape(4, 64))  1.34 us

profile of v7, /device:TPU:1, one launch (start us, length us, event | category | flops | bytes accessed | tf_op | source)
XLA Modules:
  0.0 41.0 jit_solution(1628021416870323578)
XLA Ops:
  0.0 39.7 %harmonic_sketch.1 = f32[2,128]{1,0:T(2,128)} custom-call(bf16[512,512]{1,0:T(8,128)(2,1)} %bitcast.11, s32[8,512]{1,0:T(8,128)} %mask_h.1, f32[512,64]{1,0:T(8,128)} %bitcast.12, f32[64,384]{1,0:T(8,128)} %bitcast.13, f32[1,384]{1,0:T(1,128)} %bitcast.14, f32[64,64]{1,0:T(8,128)} %cov_h.1, bf16[384,2,512]{2,1,0:T(2,128)(2,1)} %bitcast.10, ...), custom_call_target="tpu_custom_call" | custom-call | tf_op jit(solution)/shard_map/harmonic_sketch/pallas_call | solution.py:351
  39.7 1.3 %reshape.19 = f32[4,64]{1,0:T(4,128)} reshape(f32[2,128]{1,0:T(2,128)} %harmonic_sketch.1) | data formatting | bytes 2048 | tf_op jit(solution)/shard_map/reshape | solution.py:395
